TPU v7x, 128 devices: a whole 4x4x4 slice. The times are simulated.
128 devices in a mesh: obs: 8 (over z, core), lat: 16 (over x, y).
Axes of the slice: x: 4, y: 4, z: 4, core: 2. Of those that a mesh axis runs over, the one named last changes fastest.
Arguments:
- footprints: bfloat16 [8, 16, 384, 128, 128], P('obs', 'lat'), may hold values from -0.0546875 to 0.0546875
- block_rows: int32 [8, 16, 384], P('obs', 'lat'), may hold values from 0 to 31
- block_cols: int32 [8, 16, 384], P('obs', 'lat'), may hold values from 0 to 639
- block_scale: int32 [8, 16, 384], P('obs', 'lat'), may hold values from 0 to 3
- lat_width: int32 [512], replicated, may hold values from 1 to 32, as said below
- lon_width: int32 [512], replicated, may hold values from 1 to 80
- obs_weight: float32 [32768], P('obs'), may hold values from 0.3 to 3
- solution: float32 [8, 4, 512, 640], P(None, None, 'lat'), may hold values from -6 to 6
- residual: float32 [8, 4, 512, 640], P(None, None, 'lat'), may hold values from -6 to 6
- direction: float32 [8, 4, 512, 640], P(None, None, 'lat'), may hold values from -6 to 6
Outputs:
- next_solution: float32 [8, 4, 512, 640], P(None, None, 'lat')
- next_residual: float32 [8, 4, 512, 640], P(None, None, 'lat')
- next_direction: float32 [8, 4, 512, 640], P(None, None, 'lat')
Inputs may be any that keep to these rules, and one draw needn't show every extreme that they name: `lat_width`: some latitude row has band width exactly 32.
All inputs are finite; a program needn't handle non-finite values.
Results may differ from a plain program's by a relative error of at most 0.00039.
Values may be sent and summed in bfloat16 or wider, within the bound.
A program may use at most 128 MiB of HBM per device.

v0:
```python
import jax
import jax.numpy as jnp
from jax import lax
from jax.sharding import PartitionSpec as P


def lat_matrix(index_out, width_out, index_in, row_reach):
    decay_rows = row_reach / 2.0
    distance = jnp.abs(index_out[:, None] - index_in[None, :]).astype(jnp.float32)
    offsets = jnp.abs(jnp.arange(-row_reach, row_reach + 1)).astype(jnp.float32)
    limits = width_out.astype(jnp.float32)[:, None]
    weights = jnp.where(
        offsets[None, :] <= limits, jnp.exp(-2.0 * offsets / decay_rows)[None, :], 0.0
    )
    normal = jnp.sqrt(jnp.sum(weights, axis=1))
    return jnp.where(distance <= limits, jnp.exp(-distance / decay_rows), 0.0) / normal[:, None]


def lon_matrix(row_width, lon_points):
    lon_decay = lon_points / 32.0
    lon_reach = lon_points // 8
    lon_grid = jnp.arange(lon_points)
    apart_cells = jnp.abs(lon_grid[:, None] - lon_grid[None, :])
    apart_cells = jnp.minimum(apart_cells, lon_points - apart_cells).astype(jnp.float32)
    offsets = jnp.abs(jnp.arange(-lon_reach, lon_reach + 1)).astype(jnp.float32)
    limit_cells = row_width.astype(jnp.float32)
    normal = jnp.sqrt(
        jnp.sum(jnp.where(offsets <= limit_cells, jnp.exp(-2.0 * offsets / lon_decay), 0.0))
    )
    return jnp.where(apart_cells <= limit_cells, jnp.exp(-apart_cells / lon_decay), 0.0) / normal


def lon_apply(field_in, widths):
    lon_points = field_in.shape[3]

    def one_row(packed):
        slab_row, row_width = packed
        return jnp.einsum(
            "kwa,ab->kwb",
            slab_row,
            lon_matrix(row_width, lon_points),
            precision=lax.Precision.HIGHEST,
        )

    mixed_rows = lax.map(one_row, (jnp.moveaxis(field_in, 2, 0), widths))
    return jnp.moveaxis(mixed_rows, 0, 2)


def lat_apply(field_in, lat_width, adjoint_side):
    band_rows = field_in.shape[2]
    turned = lax.all_to_all(field_in, "lat", split_axis=3, concat_axis=2, tiled=True)
    lat_index = jnp.arange(turned.shape[2])
    weights = lat_matrix(lat_index, lat_width, lat_index, band_rows)
    if adjoint_side:
        weights = weights.T
    mixed_rows = jnp.einsum("ij,kwjl->kwil", weights, turned, precision=lax.Precision.HIGHEST)
    result = lax.all_to_all(mixed_rows, "lat", split_axis=2, concat_axis=3, tiled=True)
    return result


def inner_gram(left_field, right_field):
    left_rows = left_field.reshape(left_field.shape[0], -1)
    right_rows = right_field.reshape(right_field.shape[0], -1)
    return jnp.einsum("kx,jx->kj", left_rows, right_rows, precision=lax.Precision.HIGHEST)


def combine_columns(coeffs, field_in):
    return jnp.einsum("ba,bwix->awix", coeffs, field_in, precision=lax.Precision.HIGHEST)


def shards(
    footprints,
    block_rows,
    block_cols,
    block_scale,
    lat_width,
    lon_width,
    obs_weight,
    solution,
    residual,
    direction,
):
    highest = lax.Precision.HIGHEST
    rhs_count = direction.shape[0]
    band_rows = direction.shape[2]
    blocks = footprints[0, 0]
    row_list = block_rows[0, 0]
    col_list = block_cols[0, 0]
    scales = jnp.exp2(-block_scale[0, 0].astype(jnp.float32))
    block_edge = blocks.shape[1]
    row_blocks = obs_weight.shape[0] // block_edge
    lon_local = lax.dynamic_slice_in_dim(lon_width, lax.axis_index("lat") * band_rows, band_rows)
    spread_cells = lat_apply(lon_apply(direction, lon_local), lat_width, False).astype(jnp.bfloat16)
    cell_values = spread_cells.reshape(rhs_count, -1, block_edge)
    col_blocks = cell_values.shape[1]
    picked = jnp.take(cell_values, col_list, axis=1)
    partial_value = (
        jnp.einsum("nrc,knc->knr", blocks, picked, preferred_element_type=jnp.float32)
        * scales[None, :, None]
    )
    row_hot = (row_list[:, None] == jnp.arange(row_blocks)[None, :]).astype(jnp.float32)
    forward = jnp.einsum("knr,nb->kbr", partial_value, row_hot, precision=highest).reshape(
        rhs_count, -1
    )
    summed = lax.psum(forward, "lat")
    obs_values = (summed * obs_weight[None, :]).astype(jnp.bfloat16)
    slab_values = obs_values.reshape(rhs_count, row_blocks, block_edge)
    pulled = jnp.take(slab_values, row_list, axis=1)
    adjoint_terms = (
        jnp.einsum("nrc,knr->knc", blocks, pulled, preferred_element_type=jnp.float32)
        * scales[None, :, None]
    )
    col_hot = (col_list[:, None] == jnp.arange(col_blocks)[None, :]).astype(jnp.float32)
    adjoint_local = jnp.einsum("knc,nb->kbc", adjoint_terms, col_hot, precision=highest).reshape(
        direction.shape
    )
    adjoint = lax.psum(adjoint_local, "obs")
    image = direction + lon_apply(lat_apply(adjoint, lat_width, True), lon_local)
    gram_old, curvature = lax.psum(
        (inner_gram(residual, residual), inner_gram(direction, image)), "lat"
    )
    step_coef = jax.scipy.linalg.cho_solve((jnp.linalg.cholesky(curvature), True), gram_old)
    next_solution = solution + combine_columns(step_coef, direction)
    next_residual = residual - combine_columns(step_coef, image)
    gram_new = lax.psum(inner_gram(next_residual, next_residual), "lat")
    turn_coef = jax.scipy.linalg.cho_solve((jnp.linalg.cholesky(gram_old), True), gram_new)
    next_direction = next_residual + combine_columns(turn_coef, direction)
    return (next_solution, next_residual, next_direction)


def solution(mesh):
    return jax.shard_map(
        shards,
        mesh=mesh,
        in_specs=(
            P("obs", "lat", None, None, None),
            P("obs", "lat", None),
            P("obs", "lat", None),
            P("obs", "lat", None),
            P(),
            P(),
            P("obs"),
            P(None, None, "lat", None),
            P(None, None, "lat", None),
            P(None, None, "lat", None),
        ),
        out_specs=(
            P(None, None, "lat", None),
            P(None, None, "lat", None),
            P(None, None, "lat", None),
        ),
        check_vma=False,
    )
```

profile of v0, /device:TPU:0, one launch (start us, length us, event | category | flops | bytes accessed | tf_op | source)
XLA Modules:
  0.0 1130.3 jit_solution(12014234616776796775)
XLA Ops:
  7.2 4.8 copy.298
  13.0 155.9 %while.24 = (s32[]{:T(128)}, f32[32,8,4,640]{3,1,2,0:T(8,128)S(1)}, f32[32,8,4,640]{3,1,2,0:T(8,128)}, s32[32]{0:T(128)S(1)}, s32[]{:T(128)}) while((s32[]{:T(128)}, f32[32,8,4,640]{3,1,2,0:T(8,128)S(1)}, f32[32,8,4,640]{3,1,2,0:T(8,128)}, s32[32]{0:T(128)S(1)}, s32[]{:T(128)}) %tuple.77), condition=%wide.region_2.3_spmd, body=%wide.region_0.2_spmd.sunk | while | flops 161383520 | bytes 165477 | solution.py:45
  168.9 9.1 copy.203
  178.0 9.2 bitcast_bitcast_fusion
  187.2 9.5 reshape.170
  196.7 7.5 all-to-all-start
  204.4 36.9 %all-to-all-done = f32[16,1,40960]{2,1,0:T(1,128)S(1)} async-done(((f32[16,1,40960]{2,1,0:T(1,128)}), f32[16,1,40960]{2,1,0:T(1,128)S(1)}, u32[]{:S(2)}, u32[]{:S(2)}) %all-to-all-start) | async-done | bytes 2621472 | tf_op jit(solution)/shard_map/all_to_all | solution.py:51
  241.7 9.2 reduce.12
  250.9 10.9 reshape.171
  261.9 13.9 %copy.296 = f32[8,4,32,16,40]{2,3,4,1,0:T(8,128)} copy(f32[8,4,32,16,40]{2,0,1,4,3:T(8,128)} %bitcast.203) | data formatting | bytes 5242880 | tf_op jit(solution)/shard_map/all_to_all | solution.py:51
  275.7 7.8 all_to_all.49
  283.5 5.8 convolution_bitcast_fusion.1
  289.2 7.3 copy.205
  296.6 13.1 %reshape.172 = bf16[16,2,20480]{2,1,0:T(2,128)(2,1)} reshape(bf16[512,8,4,40]{3,2,1,0:T(4,128)(2,1)} %bitcast.211) | data formatting | bytes 2621440
  314.5 18.7 %all-to-all-done.1 = bf16[16,2,20480]{2,1,0:T(2,128)(2,1)S(1)} async-done(((bf16[16,2,20480]{2,1,0:T(2,128)(2,1)}), bf16[16,2,20480]{2,1,0:T(2,128)(2,1)S(1)}, u32[]{:S(2)}, u32[]{:S(2)}) %all-to-all-start.1) | async-done | bytes 1310752 | tf_op jit(solution)/shard_map/all_to_all | solution.py:57
  333.2 8.0 reshape.173
  341.3 5.5 copy.206
  346.8 4.7 convert_element_type.103
  351.5 9.8 copy.207
  361.3 8.0 convert_element_type.105
  372.0 10.0 multiply_bitcast_fusion.1
  383.6 81.5 %all-reduce.4.cloned.1.call-done = f32[8,4096]{1,0:T(8,128)} async-done(((f32[8,4096]{1,0:T(8,128)}), f32[8,4096]{1,0:T(8,128)}) %all-reduce.4.cloned.1.call-update) | async-done | bytes 131088 | tf_op jit(solution)/shard_map/psum | solution.py:105
  468.0 7.4 multiply_bitcast_fusion
  479.5 8.5 copy.211
  488.1 123.7 %all-reduce.6.cloned.1.call-done = f32[8,4,32,640]{2,1,0,3:T(4,128)} async-done(((f32[8,4,32,640]{2,1,0,3:T(4,128)}), f32[8,4,32,640]{2,1,0,3:T(4,128)}) %all-reduce.6.cloned.1.call-update) | async-done | bytes 2621456 | tf_op jit(solution)/shard_map/psum | solution.py:117
  611.8 10.9 reshape.174
  622.7 40.5 %all_to_all.63 = f32[16,1,40960]{2,1,0:T(1,128)S(1)} all-to-all(f32[16,1,40960]{2,1,0:T(1,128)} %reshape.174), channel_id=1, replica_groups=mesh['obs'=8,'lat'=16] {'lat'}, dimensions={0} | all-to-all | bytes 5242880 | tf_op jit(solution)/shard_map/all_to_all | solution.py:51
  663.2 9.2 reduce.13
  672.4 13.2 %reshape.175 = f32[640,8,4,32]{3,2,1,0:T(4,128)} reshape(f32[16,40960]{1,0:T(8,128)} %reduce.13) | data formatting | bytes 5242880
  685.6 13.9 %copy.295 = f32[8,4,32,16,40]{2,3,4,1,0:T(8,128)} copy(f32[8,4,32,16,40]{2,1,0,4,3:T(4,128)} %bitcast.205) | data formatting | bytes 5242880 | tf_op jit(solution)/shard_map/all_to_all | solution.py:51
  699.5 7.5 all_to_all.54
  707.0 6.1 convolution_bitcast_fusion
  713.1 8.3 copy.214
  721.5 14.1 %reshape.176 = f32[16,1,40960]{2,1,0:T(1,128)} reshape(f32[512,8,4,40]{3,2,1,0:T(4,128)} %bitcast.207) | data formatting | bytes 5242880
  740.2 6.1 fusion.92
  746.3 27.4 %all-to-all-done.3 = f32[16,1,40960]{2,1,0:T(1,128)} async-done(((f32[16,1,40960]{2,1,0:T(1,128)}), f32[16,1,40960]{2,1,0:T(1,128)}, u32[]{:S(2)}, u32[]{:S(2)}) %all-to-all-start.3) | async-done | bytes 2621472 | tf_op jit(solution)/shard_map/all_to_all | solution.py:57
  773.8 8.7 reduce.14
  782.5 14.9 %reshape.177 = f32[512,8,4,40]{3,2,1,0:T(4,128)} reshape(f32[16,40960]{1,0:T(8,128)S(1)} %reduce.14) | data formatting | bytes 5242880
  797.4 11.4 %copy.297 = f32[8,4,16,32,40]{4,2,3,1,0:T(8,128)} copy(f32[8,4,16,32,40]{4,1,0,3,2:T(4,128)} %bitcast.208) | data formatting | bytes 5242880 | tf_op jit(solution)/shard_map/all_to_all | solution.py:57
  808.8 7.9 all_to_all.58
  818.5 184.6 %while.25 = (s32[]{:T(128)}, f32[32,8,4,640]{3,1,2,0:T(8,128)}, f32[32,8,4,640]{3,0,2,1:T(8,128)}, s32[32]{0:T(128)S(1)}, s32[]{:T(128)}) while((s32[]{:T(128)}, f32[32,8,4,640]{3,1,2,0:T(8,128)}, f32[32,8,4,640]{3,0,2,1:T(8,128)}, s32[32]{0:T(128)S(1)}, s32[]{:T(128)}) %tuple.78), condition=%wide.region_8.9_spmd, body=%wide.region_6.8_spmd.sunk | while | flops 161383520 | bytes 328809 | solution.py:45
  1007.9 6.2 fusion.87
  1014.1 37.6 %all-reduce = (f32[8,8]{0,1:T(8,128)S(1)}, f32[8,8]{0,1:T(8,128)S(1)}) all-reduce(f32[8,8]{0,1:T(8,128)S(1)} %fusion.92, f32[8,8]{0,1:T(8,128)S(1)} %fusion.87), channel_id=1, replica_groups=mesh['obs'=8,'lat'=16] {'lat'}, use_global_device_ids=true, to_apply=%region_12.14 | all-reduce | flops 128 | bytes 1024 | tf_op jit(solution)/shard_map/psum | solution.py:119
  1055.0 6.2 copy_subtract_fusion
  1061.2 5.8 convolution_bitcast_fusion.4
  1071.7 36.0 %psum.39 = f32[8,8]{1,0:T(8,128)S(1)} all-reduce(f32[8,8]{1,0:T(8,128)S(1)} %convolution_bitcast_fusion.4), channel_id=1, replica_groups=mesh['obs'=8,'lat'=16] {'lat'}, use_global_device_ids=true, to_apply=%region_13.16 | all-reduce | flops 64 | bytes 512 | tf_op jit(solution)/shard_map/psum | solution.py:125
  1108.1 5.6 fusion.72
  1116.2 5.1 copy_add_fusion
  (297 shorter events, 305.9 us)
Async XLA Ops:
  196.7 7.5 copy-start.8
  196.7 44.5 %all-to-all-start = ((f32[16,1,40960]{2,1,0:T(1,128)}), f32[16,1,40960]{2,1,0:T(1,128)S(1)}, u32[]{:S(2)}, u32[]{:S(2)}) async-start(f32[16,1,40960]{2,1,0:T(1,128)} %reshape.170), calls=%async_computation | async-start | bytes 5242880 | tf_op jit(solution)/shard_map/all_to_all | solution.py:51
  309.7 4.7 copy-start.6
  309.7 4.7 copy-start.7
  309.7 4.7 copy-start.9
  309.7 23.6 %all-to-all-start.1 = ((bf16[16,2,20480]{2,1,0:T(2,128)(2,1)}), bf16[16,2,20480]{2,1,0:T(2,128)(2,1)S(1)}, u32[]{:S(2)}, u32[]{:S(2)}) async-start(bf16[16,2,20480]{2,1,0:T(2,128)(2,1)} %reshape.172), calls=%async_computation.1 | async-start | bytes 2621440 | tf_op jit(solution)/shard_map/all_to_all | solution.py:57
  314.3 150.8 %all-reduce.4.cloned.1.call-start = ((), (), s32[]{:S(2)}) async-start(), calls=%async_computation.4 | async-start | bytes 262144 | tf_op jit(solution)/shard_map/psum | solution.py:105
  372.0 93.2 %copy-start.5 = (f32[4096]{0:T(1024)S(1)}, f32[4096]{0:T(1024)}, u32[]{:S(2)}) copy-start(f32[4096]{0:T(1024)} %param.23) | copy-start | bytes 49156
  383.5 228.3 %all-reduce.6.cloned.1.call-start = ((), (), s32[]{:S(2)}) async-start(), calls=%async_computation.5 | async-start | bytes 20971520 | tf_op jit(solution)/shard_map/psum | solution.py:117
  735.5 4.7 copy-start.3
  735.5 38.3 %all-to-all-start.3 = ((f32[16,1,40960]{2,1,0:T(1,128)}), f32[16,1,40960]{2,1,0:T(1,128)}, u32[]{:S(2)}, u32[]{:S(2)}) async-start(f32[16,1,40960]{2,1,0:T(1,128)} %reshape.176), calls=%async_computation.3 | async-start | bytes 5242880 | tf_op jit(solution)/shard_map/all_to_all | solution.py:57
  818.5 184.6 %copy-start = (f32[8,4,32,640]{3,2,1,0:T(8,128)S(1)}, f32[8,4,32,640]{3,2,1,0:T(8,128)}, u32[]{:S(2)}) copy-start(f32[8,4,32,640]{3,2,1,0:T(8,128)} %param.26) | copy-start | bytes 7864324
  1006.4 1.5 copy-start.2
  1061.2 5.9 copy-start.1
  1113.7 2.5 copy-start.4
Sparse Core Ops, SparseCore 0:
  383.6 81.4 all-reduce.3
  488.2 123.5 all-reduce.5
where the time goes:
time: 1140 us; the launch traced here: 1130 us
  local copies, waits for them, and re-layouts  325 us (29%)
  waiting for transfers between devices  288 us (25%)
  matrix products  220 us (19%)
  blocking collectives  114 us (10%)
  loops' own time  76.2 us (7%)
  other arithmetic  75.5 us (7%)
  starting transfers between devices  16.8 us (1%)
  between operations  14.6 us (1%)
    dot_general x64, matrix products, one_row(): jnp.einsum('kwa,ab->kwb', slab_row, lon_matrix(row_width, lon_points), pr...  152 us
    psum x1, waiting for transfers between devices, shards(): adjoint = lax.psum(adjoint_local, 'obs')  124 us
    unnamed x34, local copies, waits for them, and re-layouts  117 us
    psum x1, waiting for transfers between devices, shards(): summed = lax.psum(forward, 'lat')  81.5 us
    another operation x2, loops' own time, lon_apply(): mixed_rows = lax.map(one_row, (jnp.moveaxis(field_in, 2, 0), widths))  76.2 us
    dynamic_slice x96, local copies, waits for them, and re-layouts, lon_apply(): mixed_rows = lax.map(one_row, (jnp.moveaxis(field_in, 2, 0), widths))  73.9 us
    all_to_all x2, waiting for transfers between devices, lat_apply(): lax.all_to_all(mixed_rows, 'lat', split_axis=2, concat_axis=3, tiled=True)  46.2 us
    all_to_all x5, local copies, waits for them, and re-layouts, lat_apply(): lax.all_to_all(field_in, 'lat', split_axis=3, concat_axis=2, tiled=True)  43.5 us
  transfers between devices with their start and end apart: 5, of which 5 were waited for; matrix products, arithmetic and copies ran while one was open for 1% of the time, Pallas kernels for 0%

commit v1 on v0

v1 whole, which is shorter than its diff:
```python
import functools

import jax
import jax.numpy as jnp
from jax import lax
from jax.experimental import pallas as pl
from jax.experimental.pallas import tpu as pltpu
from jax.sharding import PartitionSpec as P

MESH = pl.DeviceIdType.MESH
HIGHEST = lax.Precision.HIGHEST
F32 = jnp.float32
BF16 = jnp.bfloat16
VMEM = pltpu.VMEM
DMA = pltpu.SemaphoreType.DMA
EDGE = 128
CHIPS = 4
ANY_SPEC = pl.BlockSpec(memory_space=pl.ANY)
VMEM_SPEC = pl.BlockSpec(memory_space=pltpu.VMEM)
SMEM_SPEC = pl.BlockSpec(memory_space=pltpu.SMEM)
HALF = 320


def iota(shape, axis):
    return lax.broadcasted_iota(jnp.int32, shape, axis)


def norm_of(width, decay):
    p = jnp.exp(jnp.full_like(width, -2.0 / decay))
    return jnp.sqrt(1.0 + 2.0 * p * (1.0 - jnp.exp(width * (-2.0 / decay))) / (1.0 - p))


def down_rows(row):
    return jnp.transpose(jnp.broadcast_to(row, (EDGE, EDGE)))


def along_lon(blocks, width, decay, bits):
    rows = blocks[0].shape[0]
    count = len(blocks)
    lane = iota((rows, EDGE), 1)
    terms = width.astype(jnp.int32) + 1
    picks = [((terms >> m) & 1) == 1 for m in range(bits)]

    def shifted(values, step, sign):
        turned = [pltpu.roll(v, step if sign > 0 else EDGE - step, 1) for v in values]
        inside = lane >= step if sign > 0 else lane < EDGE - step
        return [jnp.where(inside, turned[b], turned[(b - sign) % count]) for b in range(count)]

    sides = []
    for sign in (1, -1):
        power = blocks
        total = [jnp.where(picks[0], v, 0.0) for v in blocks]
        for m in range(1, bits):
            half = 2 ** (m - 1)
            moved = shifted(power, half, sign)
            fade = jnp.exp(jnp.full((rows, EDGE), -half / decay, F32))
            power = [a + fade * c for a, c in zip(power, moved)]
            moved = shifted(total, 2 * half, sign)
            fade = fade * fade
            total = [jnp.where(picks[m], a + fade * c, t) for a, c, t in zip(power, moved, total)]
        sides.append(total)
    scale = 1.0 / norm_of(width, decay)
    return [(up + down - x) * scale for up, down, x in zip(sides[0], sides[1], blocks)]


def lat_block(offset, width, decay, present, transposed):
    r, c = iota((EDGE, EDGE), 0), iota((EDGE, EDGE), 1)
    same = (r // 32) == (c // 32)
    distance = jnp.abs((r % 32) - (c % 32) - 32 * offset).astype(F32)
    value = jnp.exp(-distance / decay) / norm_of(width, decay)
    keep = jnp.where(same & (distance <= width), value, 0.0)
    if present is not None:
        keep = jnp.where(present, keep, 0.0)
    return keep


def greet(peers):
    barrier = pltpu.get_barrier_semaphore()
    for peer in peers:
        pl.semaphore_signal(barrier, inc=1, device_id=peer, device_id_type=MESH)
    pl.semaphore_wait(barrier, len(peers))


def obs_peers(o):
    z, c = o // 2, o % 2

    def at(step, core):
        return ((z + step + CHIPS) % CHIPS) * 2 + core

    return z, c, at


def gather_over_obs(own_ref, out_ref, o, send, recv, local):
    z, c, at = obs_peers(o)
    other = 1 - c
    partner, up, down = at(0, other), at(1, c), at(-1, c)
    first, second = pl.ds(0, HALF), pl.ds(HALF, HALF)

    def copy(role, src, dst, to):
        return pltpu.make_async_remote_copy(
            src_ref=src, dst_ref=dst, send_sem=send.at[role], recv_sem=recv.at[role],
            device_id={"obs": to}, device_id_type=MESH,
        )

    def spot(step, core, rows=None):
        return out_ref.at[at(step, core)] if rows is None else out_ref.at[at(step, core), rows]

    def moved(role, step, core, rows, to):
        ref = spot(step, core, rows)
        return copy(role, ref, ref, to)

    keep = pltpu.make_async_copy(own_ref, out_ref.at[o], local)
    started = [copy(1, own_ref, out_ref.at[o], up), copy(2, own_ref, out_ref.at[o], down), copy(0, own_ref, out_ref.at[o], partner)]
    for one in started:
        one.start()
    keep.start()
    copy(1, own_ref, spot(-1, c), up).wait_recv()
    batch = [moved(3, -1, c, first, up), moved(5, -1, c, None, partner)]
    for one in batch:
        one.start()
    started += batch
    copy(2, own_ref, spot(1, c), down).wait_recv()
    batch = [moved(4, 1, c, second, down), moved(6, 1, c, None, partner)]
    for one in batch:
        one.start()
    started += batch
    copy(3, spot(2, c, first), spot(2, c, first), up).wait_recv()
    one = moved(7, 2, c, first, partner)
    one.start()
    started.append(one)
    copy(4, spot(2, c, second), spot(2, c, second), down).wait_recv()
    one = moved(8, 2, c, second, partner)
    one.start()
    started.append(one)
    copy(0, own_ref, spot(0, other), partner).wait_recv()
    moved(5, -1, other, None, partner).wait_recv()
    moved(6, 1, other, None, partner).wait_recv()
    moved(7, 2, other, first, partner).wait_recv()
    moved(8, 2, other, second, partner).wait_recv()
    for one in started:
        one.wait_send()
    keep.wait()


def halo_copies(src_ref, halo_ref, l, count, send, recv):
    result = []
    for slot, step in ((0, 1), (1, count - 1)):
        result.append(pltpu.make_async_remote_copy(
            src_ref=src_ref, dst_ref=halo_ref.at[slot], send_sem=send.at[slot], recv_sem=recv.at[slot],
            device_id={"lat": (l + step) % count}, device_id_type=MESH,
        ))
    return result


def spread_kernel(sizes, direction_ref, widths_ref, out_ref, field, smooth, wire, halo, shard, send, recv, hsend, hrecv, local):
    o, l = lax.axis_index("obs"), lax.axis_index("lat")
    bands, weeks, lon_blocks, bits, lat_decay, lon_decay = sizes
    load = pltpu.make_async_copy(direction_ref.at[o], field, local)
    load.start()
    z, c, at = obs_peers(o)
    greet([{"obs": at(0, 1 - c)}, {"obs": at(1, c)}, {"obs": at(-1, c)},
           {"lat": (l + 1) % bands}, {"lat": (l + bands - 1) % bands}])
    lon_rows = down_rows(widths_ref[0:1, :])[0:32]
    load.wait()

    @pl.loop(0, weeks)
    def _(w):
        blocks = [field[w, :, b * EDGE:(b + 1) * EDGE] for b in range(lon_blocks)]
        done = along_lon(blocks, lon_rows, lon_decay, bits)
        for b in range(lon_blocks):
            rows = pl.ds(pl.multiple_of(b * EDGE + w * 32, 32), 32)
            smooth[rows, :] = done[b]
            wire[rows, :] = done[b].astype(wire.dtype)

    copies = halo_copies(wire, halo, l, bands, hsend, hrecv)
    for one in copies:
        one.start()
    own_rows = down_rows(widths_ref[2:3, :])
    mid = lat_block(0, own_rows, lat_decay, None, False)
    low = lat_block(-1, own_rows, lat_decay, l > 0, False)
    high = lat_block(1, own_rows, lat_decay, l < bands - 1, False)
    dot = functools.partial(jnp.dot, precision=HIGHEST, preferred_element_type=F32)
    near = [dot(mid, smooth[b * EDGE:(b + 1) * EDGE, :]) for b in range(lon_blocks)]
    for one in copies:
        one.wait_recv()
    for b in range(lon_blocks):
        rows = slice(b * EDGE, (b + 1) * EDGE)
        total = near[b] + dot(low, halo[0, rows, :].astype(F32)) + dot(high, halo[1, rows, :].astype(F32))
        shard[rows, :] = total.astype(shard.dtype)
    gather_over_obs(shard, out_ref, o, send, recv, local)
    for one in copies:
        one.wait_send()


def forward_kernel(per_step, rows_ref, cols_ref, scale_ref, cells_ref, blocks_ref, out_ref, cells):
    step = pl.program_id(0)

    @pl.when(step == 0)
    def _():
        cells[...] = cells_ref[...].astype(F32)
        out_ref[...] = jnp.zeros_like(out_ref)

    def one(n, carry):
        at = step * per_step + n
        col = cols_ref[at]
        start = (col % 5) * EDGE + col // 5
        picked = cells[pl.ds(start, 8, stride=640), :].astype(BF16)
        value = lax.dot_general(picked, blocks_ref[n], (((1,), (1,)), ((), ())), preferred_element_type=F32)
        factor = (8 >> scale_ref[at]).astype(F32) * 0.125
        row = rows_ref[at]
        out_ref[row] = out_ref[row] + value * factor
        return carry

    lax.fori_loop(0, per_step, one, 0, unroll=8)


def adjoint_kernel(per_step, rows_ref, cols_ref, scale_ref, values_ref, blocks_ref, out_ref):
    step = pl.program_id(0)

    @pl.when(step == 0)
    def _():
        out_ref[...] = jnp.zeros_like(out_ref)

    def one(n, carry):
        at = step * per_step + n
        col = cols_ref[at]
        start = (col % 5) * EDGE + col // 5
        value = jnp.dot(values_ref[rows_ref[at]], blocks_ref[n], preferred_element_type=F32)
        factor = (8 >> scale_ref[at]).astype(F32) * 0.125
        place = pl.ds(start, 8, stride=640)
        out_ref[place, :] = out_ref[place, :] + value * factor
        return carry

    lax.fori_loop(0, per_step, one, 0, unroll=8)


def sum_bands_kernel(bands, part_ref, weight_ref, out_ref, got, shard, send, recv, send2, recv2):
    l = lax.axis_index("lat")
    share = part_ref.shape[0] // bands
    greet([{"lat": (l + d) % bands} for d in range(1, bands)])
    mine = pl.ds(l * share, share)

    def first(d):
        peer = (l + d) % bands
        return pltpu.make_async_remote_copy(
            src_ref=part_ref.at[pl.ds(peer * share, share)], dst_ref=got.at[d], send_sem=send.at[d], recv_sem=recv.at[d],
            device_id={"lat": peer}, device_id_type=MESH,
        )

    def second(d, owner):
        return pltpu.make_async_remote_copy(
            src_ref=shard, dst_ref=out_ref.at[pl.ds(owner * share, share)], send_sem=send2.at[d], recv_sem=recv2.at[d],
            device_id={"lat": (l + d) % bands}, device_id_type=MESH,
        )

    for d in range(1, bands):
        first(d).start()
    total = part_ref[mine]
    for d in range(1, bands):
        first(d).wait_recv()
        total = total + got[d]
    weight = weight_ref[mine]
    shard[...] = (total * weight).astype(shard.dtype)
    for d in range(1, bands):
        second(d, l).start()
    out_ref[mine] = shard[...]
    for d in range(1, bands):
        second(d, (l + bands - d) % bands).wait_recv()
    for d in range(1, bands):
        first(d).wait_send()
        second(d, l).wait_send()


def image_kernel(sizes, part_ref, widths_ref, out_ref, own, there, chip, got_half, got_full, band, halo, shard,
                 send, recv, hsend, hrecv, psend, precv, rsend, rrecv, load, local):
    o, l = lax.axis_index("obs"), lax.axis_index("lat")
    bands, weeks, lon_blocks, bits, lat_decay, lon_decay = sizes
    z, c, at = obs_peers(o)
    other = 1 - c
    partner, up, down = at(0, other), at(1, c), at(-1, c)
    greet([{"obs": partner}, {"obs": up}, {"obs": down},
           {"lat": (l + 1) % bands}, {"lat": (l + bands - 1) % bands}])
    order = (2, 1, 3, 0)

    def swap(s):
        return pltpu.make_async_remote_copy(
            src_ref=part_ref.at[at(s, other)], dst_ref=there.at[s], send_sem=psend.at[s], recv_sem=precv.at[s],
            device_id={"obs": partner}, device_id_type=MESH,
        )

    def fetch(s):
        return pltpu.make_async_copy(part_ref.at[at(s, c)], own.at[s], load.at[s])

    for s in order:
        swap(s).start()
        fetch(s).start()

    def ring(role, src, dst, to):
        return pltpu.make_async_remote_copy(
            src_ref=src, dst_ref=dst, send_sem=rsend.at[role], recv_sem=rrecv.at[role],
            device_id={"obs": to}, device_id_type=MESH,
        )

    def arrive(s):
        swap(s).wait_recv()
        fetch(s).wait()

    first, second = pl.ds(0, HALF), pl.ds(HALF, HALF)
    far_up = ring(0, chip.at[2, first], got_half.at[0], up)
    far_down = ring(1, chip.at[2, second], got_half.at[1], down)
    near_up = ring(2, chip.at[1], got_full.at[0], up)
    near_down = ring(3, chip.at[3], got_full.at[1], down)
    arrive(2)
    chip[2] = (own[2] + there[2]).astype(chip.dtype)
    far_up.start()
    far_down.start()
    arrive(1)
    chip[1, HALF:, :] = (own[1, HALF:, :] + there[1, HALF:, :]).astype(chip.dtype)
    arrive(3)
    chip[3, :HALF, :] = (own[3, :HALF, :] + there[3, :HALF, :]).astype(chip.dtype)
    far_up.wait_recv()
    chip[1, :HALF, :] = (own[1, :HALF, :] + there[1, :HALF, :] + got_half[0].astype(F32)).astype(chip.dtype)
    near_up.start()
    far_down.wait_recv()
    chip[3, HALF:, :] = (own[3, HALF:, :] + there[3, HALF:, :] + got_half[1].astype(F32)).astype(chip.dtype)
    near_down.start()
    arrive(0)
    own[0] = own[0] + there[0]
    dot = functools.partial(jnp.dot, precision=HIGHEST, preferred_element_type=F32)
    low = lat_block(-1, widths_ref[1:2, :], lat_decay, l > 0, True)
    mid = lat_block(0, widths_ref[2:3, :], lat_decay, None, True)
    high = lat_block(1, widths_ref[3:4, :], lat_decay, l < bands - 1, True)
    near_up.wait_recv()
    near_down.wait_recv()
    total = own[0] + got_full[0].astype(F32) + got_full[1].astype(F32)
    own[0] = total
    band[...] = total.astype(band.dtype)
    copies = halo_copies(band, halo, l, bands, hsend, hrecv)
    for one in copies:
        one.start()
    near = [dot(mid, own[0, b * EDGE:(b + 1) * EDGE, :]) for b in range(lon_blocks)]
    for one in copies:
        one.wait_recv()
    for b in range(lon_blocks):
        rows = slice(b * EDGE, (b + 1) * EDGE)
        own[1, rows, :] = near[b] + dot(low, halo[0, rows, :].astype(F32)) + dot(high, halo[1, rows, :].astype(F32))
    lon_rows = down_rows(widths_ref[0:1, :])[0:32]

    @pl.loop(0, weeks)
    def _(w):
        places = [pl.ds(pl.multiple_of(b * EDGE + w * 32, 32), 32) for b in range(lon_blocks)]
        done = along_lon([own[1, place, :] for place in places], lon_rows, lon_decay, bits)
        for place, value in zip(places, done):
            shard[place, :] = value.astype(shard.dtype)

    gather_over_obs(shard, out_ref, o, send, recv, local)
    for one in copies + [far_up, far_down, near_up, near_down]:
        one.wait_send()
    for s in order:
        swap(s).wait_send()


def gram_kernel(k, residual_ref, direction_ref, change_ref, out_ref, sums):
    step = pl.program_id(0)
    lon_blocks = change_ref.shape[1]

    @pl.when(step == 0)
    def _():
        sums[...] = jnp.zeros_like(sums)

    def one(b, carry):
        lanes = pl.ds(pl.multiple_of(b * EDGE, EDGE), EDGE)
        res = [residual_ref[i, 0, :, lanes] for i in range(k)]
        dire = [direction_ref[i, 0, :, lanes] for i in range(k)]
        img = [dire[i] + change_ref[i, b].astype(F32) for i in range(k)]

        def add(t, i, j, x, y):
            sums[t, i, j] = sums[t, i, j] + jnp.sum((x * y).reshape(4, 8, EDGE), axis=0)

        for i in range(k):
            for j in range(k):
                if i <= j:
                    add(0, i, j, res[i], res[j])
                    add(3, i, j, img[i], img[j])
                add(1, i, j, dire[i], img[j])
                add(2, i, j, img[i], res[j])
        return carry

    lax.fori_loop(0, lon_blocks, one, 0)

    @pl.when(step == pl.num_programs(0) - 1)
    def _():
        lane, row = iota((k, EDGE), 1), iota((k, EDGE), 0)
        result = jnp.zeros((k, EDGE), F32)
        for t in range(4):
            for i in range(k):
                line = jnp.sum(jnp.sum(sums[t, i], axis=1), axis=1, keepdims=True)
                line = jnp.broadcast_to(line, (k, EDGE))
                result = jnp.where(lane == t * k + i, line, result)
        out_ref[...] = result


def flip(x):
    square = jnp.concatenate([x, jnp.zeros((EDGE - 8, EDGE), F32)], axis=0)
    return jnp.transpose(square)[:8, :]


def product(x, y):
    return sum(jnp.broadcast_to(x[:, i:i + 1], (8, EDGE)) * jnp.broadcast_to(y[i:i + 1, :], (8, EDGE)) for i in range(8))


def solve(a, b):
    row = iota((8, EDGE), 0)
    for p in range(8):
        line = jnp.broadcast_to(a[p:p + 1, :], (8, EDGE))
        line_b = jnp.broadcast_to(b[p:p + 1, :], (8, EDGE))
        column = jnp.broadcast_to(a[:, p:p + 1], (8, EDGE))
        inverse = 1.0 / jnp.broadcast_to(a[p:p + 1, p:p + 1], (8, EDGE))
        ratio = column * inverse
        here = row == p
        a = jnp.where(here, line * inverse, a - ratio * line)
        b = jnp.where(here, line_b * inverse, b - ratio * line_b)
    return b


def solve_kernel(bands, part_ref, out_ref, got, send, recv):
    l = lax.axis_index("lat")
    greet([{"lat": (l + d) % bands} for d in range(1, bands)])

    def to(d):
        return pltpu.make_async_remote_copy(
            src_ref=part_ref, dst_ref=got.at[l], send_sem=send.at[d], recv_sem=recv.at[d],
            device_id={"lat": (l + d) % bands}, device_id_type=MESH,
        )

    for d in range(1, bands):
        to(d).start()
    got[l] = part_ref[...]
    for d in range(1, bands):
        to(d).wait_recv()
    total = got[0]
    for d in range(1, bands):
        total = total + got[d]
    lane, row = iota((8, EDGE), 1), iota((8, EDGE), 0)
    parts = []
    for t in range(4):
        moved = total if t == 0 else pltpu.roll(total, EDGE - 8 * t, 1)
        parts.append(jnp.where(lane < 8, moved, 0.0))

    def full(x):
        low = jnp.where(lane <= row, x, 0.0)
        return low + flip(jnp.where(lane < row, x, 0.0))

    gram_old, image_image = full(parts[0]), full(parts[3])
    curvature = 0.5 * (parts[1] + flip(parts[1]))
    residual_image = parts[2]
    step = solve(curvature, gram_old)
    cross = product(residual_image, step)
    gram_new = gram_old - cross - flip(cross) + product(flip(step), product(image_image, step))
    turn = solve(gram_old, gram_new)
    out_ref[...] = jnp.where(lane < 8, step, 0.0) + pltpu.roll(jnp.where(lane < 8, turn, 0.0), 8, 1)
    for d in range(1, bands):
        to(d).wait_send()


def update_kernel(k, coef_ref, solution_ref, residual_ref, direction_ref, change_ref, sol_out, res_out, dir_out):
    lon_blocks = change_ref.shape[1]

    def one(b, carry):
        lanes = pl.ds(pl.multiple_of(b * EDGE, EDGE), EDGE)
        for r in range(4):
            rows = slice(r * 8, r * 8 + 8)
            dire = [direction_ref[i, 0, rows, lanes] for i in range(k)]
            img = [dire[i] + change_ref[i, b, rows, :].astype(F32) for i in range(k)]
            for a in range(k):
                forth = sum(coef_ref[i, a] * dire[i] for i in range(k))
                back = sum(coef_ref[i, a] * img[i] for i in range(k))
                turn = sum(coef_ref[i, k + a] * dire[i] for i in range(k))
                left = residual_ref[a, 0, rows, lanes] - back
                sol_out[a, 0, rows, lanes] = solution_ref[a, 0, rows, lanes] + forth
                res_out[a, 0, rows, lanes] = left
                dir_out[a, 0, rows, lanes] = left + turn
        return carry

    lax.fori_loop(0, lon_blocks, one, 0)


WIRE_OUT = F32
WIRE_SUM = F32
WIRE_BACK = F32
WIRE_IMAGE = F32


def params(collective=None, limit=None):
    extra = {} if collective is None else {"collective_id": collective, "has_side_effects": True}
    return pltpu.CompilerParams(vmem_limit_bytes=limit or (48 << 20), **extra)


def shards(bands, footprints, block_rows, block_cols, block_scale, lat_width, lon_width, obs_weight, solution, residual, direction):
    k, weeks, band_rows, nlon = direction.shape
    blocks = footprints.shape[2]
    lon_blocks = nlon // EDGE
    field_rows = weeks * band_rows * lon_blocks
    assert (k, weeks, band_rows, field_rows) == (8, 4, 32, 2 * HALF)
    row_blocks = obs_weight.shape[0] // EDGE
    sizes = (bands, weeks, lon_blocks, (nlon // 8 + 1).bit_length(), band_rows / 2.0, nlon / 32.0)
    l = lax.axis_index("lat")
    around = jnp.pad(lat_width.reshape(bands, band_rows), ((1, 1), (0, 0)))
    near = jnp.concatenate([
        lax.dynamic_slice_in_dim(lon_width.reshape(bands, band_rows), l, 1),
        lax.dynamic_slice_in_dim(around, l, 3),
    ])
    widths = jnp.pad(jnp.tile(near, (1, weeks)), ((0, 4), (0, 0))).astype(F32)
    rows, cols, scale = block_rows.reshape(blocks), block_cols.reshape(blocks), block_scale.reshape(blocks)
    field = (field_rows, EDGE)

    cells = pl.pallas_call(
        functools.partial(spread_kernel, sizes),
        out_shape=jax.ShapeDtypeStruct((k, *field), BF16),
        in_specs=[ANY_SPEC, VMEM_SPEC],
        out_specs=ANY_SPEC,
        scratch_shapes=[
            VMEM((weeks, band_rows, nlon), F32), VMEM(field, F32), VMEM(field, WIRE_OUT), VMEM((2, *field), WIRE_OUT),
            VMEM(field, BF16), DMA((9,)), DMA((9,)), DMA((2,)), DMA((2,)), DMA(()),
        ],
        compiler_params=params(1),
        name="spread",
    )(direction, widths)

    per_step = 48
    smem = [SMEM_SPEC] * 3
    block_spec = pl.BlockSpec((None, None, per_step, EDGE, EDGE), lambda i: (0, 0, i, 0, 0))
    forward = pl.pallas_call(
        functools.partial(forward_kernel, per_step),
        grid=(blocks // per_step,),
        out_shape=jax.ShapeDtypeStruct((row_blocks, k, EDGE), F32),
        in_specs=smem + [pl.BlockSpec((k * field_rows, EDGE), lambda i: (0, 0)), block_spec],
        out_specs=pl.BlockSpec((row_blocks, k, EDGE), lambda i: (0, 0, 0)),
        scratch_shapes=[VMEM((k * field_rows, EDGE), F32)],
        compiler_params=params(),
        name="forward",
    )(rows, cols, scale, cells.reshape(k * field_rows, EDGE), footprints)

    share = row_blocks // bands
    values = pl.pallas_call(
        functools.partial(sum_bands_kernel, bands),
        out_shape=jax.ShapeDtypeStruct((row_blocks, k, EDGE), BF16),
        in_specs=[VMEM_SPEC, VMEM_SPEC],
        out_specs=VMEM_SPEC,
        scratch_shapes=[
            VMEM((bands, share, k, EDGE), F32), VMEM((share, k, EDGE), BF16),
            DMA((bands,)), DMA((bands,)), DMA((bands,)), DMA((bands,)),
        ],
        compiler_params=params(2),
        name="sum_bands",
    )(forward, obs_weight.reshape(row_blocks, 1, EDGE))

    part = pl.pallas_call(
        functools.partial(adjoint_kernel, per_step),
        grid=(blocks // per_step,),
        out_shape=jax.ShapeDtypeStruct((k * field_rows, EDGE), F32),
        in_specs=smem + [pl.BlockSpec((row_blocks, k, EDGE), lambda i: (0, 0, 0)), block_spec],
        out_specs=pl.BlockSpec((k * field_rows, EDGE), lambda i: (0, 0)),
        compiler_params=params(),
        name="adjoint",
    )(rows, cols, scale, values, footprints)

    half = (HALF, EDGE)
    change = pl.pallas_call(
        functools.partial(image_kernel, sizes),
        out_shape=jax.ShapeDtypeStruct((k, *field), WIRE_IMAGE),
        in_specs=[ANY_SPEC, VMEM_SPEC],
        out_specs=ANY_SPEC,
        scratch_shapes=[
            VMEM((CHIPS, *field), F32), VMEM((CHIPS, *field), F32), VMEM((CHIPS, *field), WIRE_SUM),
            VMEM((2, *half), WIRE_SUM), VMEM((2, *field), WIRE_SUM), VMEM(field, WIRE_BACK), VMEM((2, *field), WIRE_BACK),
            VMEM(field, WIRE_IMAGE),
            DMA((9,)), DMA((9,)), DMA((2,)), DMA((2,)), DMA((CHIPS,)), DMA((CHIPS,)), DMA((CHIPS,)), DMA((CHIPS,)),
            DMA((CHIPS,)), DMA(()),
        ],
        compiler_params=params(3),
        name="image",
    )(part.reshape(k, *field), widths)

    change = change.reshape(k, lon_blocks, EDGE, EDGE)
    native = pl.BlockSpec((k, 1, band_rows, nlon), lambda w: (0, w, 0, 0))
    packed = pl.BlockSpec((k, lon_blocks, band_rows, EDGE), lambda w: (0, 0, w, 0))
    gram = pl.pallas_call(
        functools.partial(gram_kernel, k),
        grid=(weeks,),
        out_shape=jax.ShapeDtypeStruct((k, EDGE), F32),
        in_specs=[native, native, packed],
        out_specs=pl.BlockSpec((k, EDGE), lambda w: (0, 0)),
        scratch_shapes=[VMEM((4, k, k, 8, EDGE), F32)],
        compiler_params=params(),
        name="gram",
    )(residual, direction, change)

    coef = pl.pallas_call(
        functools.partial(solve_kernel, bands),
        out_shape=jax.ShapeDtypeStruct((k, EDGE), F32),
        in_specs=[VMEM_SPEC],
        out_specs=VMEM_SPEC,
        scratch_shapes=[VMEM((bands, k, EDGE), F32), DMA((bands,)), DMA((bands,))],
        compiler_params=params(4),
        name="solve",
    )(gram)

    return pl.pallas_call(
        functools.partial(update_kernel, k),
        grid=(weeks,),
        out_shape=[jax.ShapeDtypeStruct(direction.shape, F32)] * 3,
        in_specs=[SMEM_SPEC, native, native, native, packed],
        out_specs=[native] * 3,
        compiler_params=params(),
        name="update",
    )(coef, solution, residual, direction, change)


def solution(mesh):
    assert mesh.shape["obs"] == 2 * CHIPS
    three = (P(None, None, "lat", None),) * 3
    blocks = P("obs", "lat", None)
    return jax.shard_map(
        functools.partial(shards, mesh.shape["lat"]),
        mesh=mesh,
        in_specs=(P("obs", "lat", None, None, None), blocks, blocks, blocks, P(), P(), P("obs"), *three),
        out_specs=three,
        check_vma=False,
    )
```

time: 1140 us -> 156 us (0.14)
  local copies, waits for them, and re-layouts: 325 us -> 4.88 us
  waiting for transfers between devices: 288 us -> 0 us
  matrix products: 220 us -> 0 us
  Pallas kernels: 0 us -> 147 us
  blocking collectives: 114 us -> 0 us
  loops' own time: 76.2 us -> 0 us
  other arithmetic: 75.5 us -> 2.11 us
  starting transfers between devices: 16.8 us -> 0 us
  between operations: 14.6 us -> 0.74 us
    dot_general x76 -> x0, matrix products: 219 us -> none  [the longest x64 152 us: one_row(): jnp.einsum('kwa,ab->kwb', slab_row, lon_matrix(row_width, lon_points), pr...]
    psum x2 -> x0, waiting for transfers between devices: 205 us -> none  [the longest x1 124 us: shards(): adjoint = lax.psum(adjoint_local, 'obs')]
    pallas_call x0 -> x8, Pallas kernels: none -> 147 us  [the longest x1 48.5 us: shards(): pl.pallas_call(functools.partial(image_kernel, sizes), out_shape=jax.Shap...]
    unnamed x34 -> x12, local copies, waits for them, and re-layouts: 117 us -> 3.26 us
    all_to_all x3 -> x0, waiting for transfers between devices: 83.1 us -> none  [the longest x2 46.2 us: lat_apply(): lax.all_to_all(mixed_rows, 'lat', split_axis=2, concat_axis=3, tiled=True)]
    another operation x2 -> x0, loops' own time: 76.2 us -> none  [lon_apply(): mixed_rows = lax.map(one_row, (jnp.moveaxis(field_in, 2, 0), widths))]
    dynamic_slice x97 -> x2, local copies, waits for them, and re-layouts: 74.6 us -> 0.02 us  [the longest x1 0.01 us: shards(): lax.dynamic_slice_in_dim(around, l, 3)]
    psum x2 -> x0, blocking collectives: 73.6 us -> none  [the longest x1 37.6 us: shards(): lax.psum((inner_gram(residual, residual), inner_gram(direction, image)),...]
  transfers between devices with their start and end apart: 5 -> 0, of which waited for: 5 -> 0; matrix products, arithmetic and copies ran while one was open for 1% -> 0% of each run, Pallas kernels for 0% -> 0%
where the time goes in v1:
time: 156 us; the launch traced here: 155 us
  Pallas kernels  147 us (94%)
  local copies, waits for them, and re-layouts  4.88 us (3%)
  other arithmetic  2.11 us (1%)
    pallas_call x1, Pallas kernels, shards(): pl.pallas_call(functools.partial(image_kernel, sizes), out_shape=jax.Shap...  48.5 us
    pallas_call x1, Pallas kernels, shards(): pl.pallas_call(functools.partial(spread_kernel, sizes), out_shape=jax.Sha...  30.5 us
    pallas_call x1, Pallas kernels, shards(): pl.pallas_call(functools.partial(sum_bands_kernel, bands), out_shape=jax....  14.8 us
    pallas_call x1, Pallas kernels, shards(): pl.pallas_call(functools.partial(forward_kernel, per_step), grid=(blocks...  14 us
    pallas_call x1, Pallas kernels, shards(): pl.pallas_call(functools.partial(adjoint_kernel, per_step), grid=(blocks...  12.9 us
    pallas_call x1, Pallas kernels, shards(): pl.pallas_call(functools.partial(solve_kernel, bands), out_shape=jax.Shap...  10.1 us
    pallas_call x1, Pallas kernels, shards(): pl.pallas_call(functools.partial(update_kernel, k), grid=(weeks,), out_sh...  9.19 us
    pallas_call x1, Pallas kernels, shards(): pl.pallas_call(functools.partial(gram_kernel, k), grid=(weeks,), out_shap...  6.7 us

profile of v1, /device:TPU:0, one launch (start us, length us, event | category | flops | bytes accessed | tf_op | source)
XLA Modules:
  0.0 154.6 jit_solution(15162839060479093692)
XLA Ops:
  0.6 0.7 reduce.rows_ref
  1.3 0.7 reduce.1.cols_ref
  2.0 0.7 reduce.2.scale_ref
  2.7 0.8 reshape.41
  3.5 0.8 reshape.40
  4.3 0.1 tile.10
  4.4 0.0 copy-start
  4.4 1.7 %copy-done = f32[8,4,32,640]{3,2,1,0:T(8,128)S(1)} copy-done((f32[8,4,32,640]{3,2,1,0:T(8,128)S(1)}, f32[8,4,32,640]{3,2,1,0:T(8,128)}, u32[]{:S(2)}) %copy-start) | copy-done | bytes 2621464
  6.1 30.5 %spread.1 = bf16[8,640,128]{2,1,0:T(8,128)(2,1)S(1)} custom-call(f32[8,4,32,640]{3,2,1,0:T(8,128)S(1)} %copy-done, f32[8,128]{1,0:T(8,128)S(1)} %pad_convert_fusion.widths_ref), custom_call_target="tpu_custom_call" | custom-call | tf_op jit(solution)/shard_map/spread/pallas_call | solution.py:517
  36.6 0.0 copy-start.5
  36.6 14.0 %forward.1.part_ref = f32[32,8,128]{2,1,0:T(8,128)S(1)} custom-call(s32[384]{0:T(512)S(1)} %reduce.rows_ref, s32[384]{0:T(512)S(1)} %reduce.1.cols_ref, s32[384]{0:T(512)S(1)} %reduce.2.scale_ref, bf16[5120,128]{1,0:T(8,128)(2,1)S(1)} %bitcast.7, bf16[1,1,384,128,128]{4,3,2,1,0:T(8,128)(2,1)} %blocks_ref.3), custom_call_target="tpu_custom_call" | custom-call | tf_op jit(solution)/shard_map/forward/pallas_call | solution.py:533
  50.7 0.0 copy-done.5
  50.7 14.8 %sum_bands.1.values_ref = bf16[32,8,128]{2,1,0:T(8,128)(2,1)S(1)} custom-call(f32[32,8,128]{2,1,0:T(8,128)S(1)} %forward.1.part_ref, f32[32,1,128]{2,1,0:T(1,128)S(1)} %bitcast.8), custom_call_target="tpu_custom_call" | custom-call | tf_op jit(solution)/shard_map/sum_bands/pallas_call | solution.py:545
  65.5 12.9 %adjoint.1 = f32[5120,128]{1,0:T(8,128)S(1)} custom-call(s32[384]{0:T(512)S(1)} %reduce.rows_ref, s32[384]{0:T(512)S(1)} %reduce.1.cols_ref, s32[384]{0:T(512)S(1)} %reduce.2.scale_ref, bf16[32,8,128]{2,1,0:T(8,128)(2,1)S(1)} %sum_bands.1.values_ref, bf16[1,1,384,128,128]{4,3,2,1,0:T(8,128)(2,1)} %blocks_ref.3), custom_call_target="tpu_custom_call" | custom-call | tf_op jit(solution)/shard_map/adjoint/pallas_call | solution.py:558
  78.5 0.0 copy-start.1
  78.5 0.0 copy-start.3
  78.5 48.5 %image.1 = f32[8,640,128]{2,1,0:T(8,128)S(1)} custom-call(f32[8,640,128]{2,1,0:T(8,128)S(1)} %bitcast.6, f32[8,128]{1,0:T(8,128)S(1)} %pad_convert_fusion.widths_ref), custom_call_target="tpu_custom_call" | custom-call | tf_op jit(solution)/shard_map/image/pallas_call | solution.py:569
  127.0 0.0 copy-start.2
  127.0 1.5 copy-done.2
  128.5 0.0 copy-done.1
  128.5 0.0 copy-done.3
  128.5 0.0 copy-start.4
  128.5 6.7 %gram.1.part_ref = f32[8,128]{1,0:T(8,128)S(1)} custom-call(f32[8,4,32,640]{3,2,1,0:T(8,128)S(1)} %copy-done.3, f32[8,4,32,640]{3,2,1,0:T(8,128)S(1)} %copy-done.1, f32[8,5,128,128]{3,2,1,0:T(8,128)} %bitcast.4), custom_call_target="tpu_custom_call" | custom-call | tf_op jit(solution)/shard_map/gram/pallas_call | solution.py:588
  135.2 10.1 %solve.1.coef_ref = f32[8,128]{1,0:T(8,128)S(1)} custom-call(f32[8,128]{1,0:T(8,128)S(1)} %gram.1.part_ref), custom_call_target="tpu_custom_call" | custom-call | tf_op jit(solution)/shard_map/solve/pallas_call | solution.py:599
  145.3 0.0 copy-done.4
  145.4 9.2 %update.1 = (f32[8,4,32,640]{3,2,1,0:T(8,128)}, f32[8,4,32,640]{3,2,1,0:T(8,128)}, f32[8,4,32,640]{3,2,1,0:T(8,128)}) custom-call(f32[8,128]{1,0:T(8,128)S(1)} %solve.1.coef_ref, f32[8,4,32,640]{3,2,1,0:T(8,128)S(1)} %copy-done.4, f32[8,4,32,640]{3,2,1,0:T(8,128)S(1)} %copy-done.3, f32[8,4,32,640]{3,2,1,0:T(8,128)} %direction_ref.5, f32[8,5,128,128]{3,2,1,0:T(8,128)} %bitcast.5), custom_call_target="tpu_custom_call" | custom-call | tf_op jit(solution)/shard_map/update/pallas_call | solution.py:609
  (5 shorter events, 0.0 us)
Async XLA Ops:
  4.4 1.7 %copy-start = (f32[8,4,32,640]{3,2,1,0:T(8,128)S(1)}, f32[8,4,32,640]{3,2,1,0:T(8,128)}, u32[]{:S(2)}) copy-start(f32[8,4,32,640]{3,2,1,0:T(8,128)} %direction_ref.5) | copy-start | bytes 7864324
  36.6 14.1 %copy-start.5 = (f32[4096]{0:T(1024)S(1)}, f32[4096]{0:T(1024)}, u32[]{:S(2)}) copy-start(f32[4096]{0:T(1024)} %param.16) | copy-start | bytes 49156
  78.5 50.0 %copy-start.1 = (f32[8,4,32,640]{3,2,1,0:T(8,128)S(1)}, f32[8,4,32,640]{3,2,1,0:T(8,128)}, u32[]{:S(2)}) copy-start(f32[8,4,32,640]{3,2,1,0:T(8,128)} %direction_ref.5) | copy-start | bytes 7864324
  78.5 50.0 %copy-start.3 = (f32[8,4,32,640]{3,2,1,0:T(8,128)S(1)}, f32[8,4,32,640]{3,2,1,0:T(8,128)}, u32[]{:S(2)}) copy-start(f32[8,4,32,640]{3,2,1,0:T(8,128)} %residual_ref.3) | copy-start | bytes 7864324
  127.0 1.5 copy-start.2
  128.5 16.9 %copy-start.4 = (f32[8,4,32,640]{3,2,1,0:T(8,128)S(1)}, f32[8,4,32,640]{3,2,1,0:T(8,128)}, u32[]{:S(2)}) copy-start(f32[8,4,32,640]{3,2,1,0:T(8,128)} %solution_ref.1) | copy-start | bytes 7864324

commit v2 on v1

v2 whole, which is shorter than its diff:
```python
import functools

import jax
import jax.numpy as jnp
from jax import lax
from jax.experimental import pallas as pl
from jax.experimental.pallas import tpu as pltpu
from jax.sharding import PartitionSpec as P

MESH = pl.DeviceIdType.MESH
HIGHEST = lax.Precision.HIGHEST
F32 = jnp.float32
BF16 = jnp.bfloat16
VMEM = pltpu.VMEM
DMA = pltpu.SemaphoreType.DMA
EDGE = 128
CHIPS = 4
ANY_SPEC = pl.BlockSpec(memory_space=pl.ANY)
VMEM_SPEC = pl.BlockSpec(memory_space=pltpu.VMEM)
SMEM_SPEC = pl.BlockSpec(memory_space=pltpu.SMEM)
BAND = 32
WEEK = 160
CODED = WEEK + 16
FIELD = 640
STEP = FIELD + 1
TOP = 32000.0


def iota(shape, axis):
    return lax.broadcasted_iota(jnp.int32, shape, axis)


def norm_of(width, decay):
    p = jnp.exp(jnp.full_like(width, -2.0 / decay))
    return jnp.sqrt(1.0 + 2.0 * p * (1.0 - jnp.exp(width * (-2.0 / decay))) / (1.0 - p))


def down_rows(row):
    return jnp.transpose(jnp.broadcast_to(row, (EDGE, EDGE)))


def along_lon(blocks, width, decay, bits):
    rows = blocks[0].shape[0]
    count = len(blocks)
    lane = iota((rows, EDGE), 1)
    terms = width.astype(jnp.int32) + 1
    picks = [((terms >> m) & 1) == 1 for m in range(bits)]

    def shifted(values, step, sign):
        turned = [pltpu.roll(v, step if sign > 0 else EDGE - step, 1) for v in values]
        inside = lane >= step if sign > 0 else lane < EDGE - step
        return [jnp.where(inside, turned[b], turned[(b - sign) % count]) for b in range(count)]

    sides = []
    for sign in (1, -1):
        power = blocks
        total = [jnp.where(picks[0], v, 0.0) for v in blocks]
        for m in range(1, bits):
            half = 2 ** (m - 1)
            moved = shifted(power, half, sign)
            fade = jnp.exp(jnp.full((rows, EDGE), -half / decay, F32))
            power = [a + fade * c for a, c in zip(power, moved)]
            moved = shifted(total, 2 * half, sign)
            fade = fade * fade
            total = [jnp.where(picks[m], a + fade * c, t) for a, c, t in zip(power, moved, total)]
        sides.append(total)
    scale = 1.0 / norm_of(width, decay)
    return [(up + down - x) * scale for up, down, x in zip(sides[0], sides[1], blocks)]


def lat_rows(widths, reach, l, bands, across):
    r, c = iota((BAND, EDGE), 0), iota((BAND, EDGE), 1)
    width = widths[1:2, :] if across else down_rows(widths[1:2, :])[BAND:2 * BAND]
    distance = jnp.abs(r - c + BAND).astype(F32)
    low = jnp.where(l > 0, 0, BAND)
    high = jnp.where(l < bands - 1, 3 * BAND, 2 * BAND)
    value = jnp.exp(-distance / reach) / norm_of(width, reach)
    return jnp.where((distance <= width) & (c >= low) & (c < high), value, 0.0)


def mix_rows(weights, stacks):
    weights = weights[:, :3 * BAND]
    large = weights.astype(BF16)
    both = jnp.concatenate([large, (weights - large.astype(F32)).astype(BF16)], axis=0)
    stack = jnp.concatenate(stacks, axis=1)
    first = stack.astype(BF16)
    second = (stack - first.astype(F32)).astype(BF16)
    main = jnp.dot(both, first, preferred_element_type=F32)
    total = main[:BAND] + (main[BAND:] + jnp.dot(large, second, preferred_element_type=F32))
    return [total[:, b * EDGE:(b + 1) * EDGE] for b in range(len(stacks))]


def encode(ref, blocks):
    row = iota((16, EDGE), 0)
    powers = jnp.zeros((16, EDGE), F32)
    for b, value in enumerate(blocks):
        top = jnp.max(jnp.abs(value), axis=0, keepdims=True)
        power = jnp.ceil(jnp.log2(jnp.maximum(top, 1e-30)))
        whole = jnp.round(value * (jnp.exp2(-power) * TOP))
        ref[b * BAND:(b + 1) * BAND, :] = whole.astype(jnp.int32).astype(jnp.int16)
        powers = jnp.where(row == b, jnp.broadcast_to(power, (16, EDGE)), powers)
    ref[WEEK:CODED, :] = powers.astype(jnp.int32).astype(jnp.int16)


def scales_of(ref, count):
    powers = jnp.exp2(ref[WEEK:CODED, :].astype(jnp.int32).astype(F32)) * (1.0 / TOP)
    return [powers[b:b + 1, :] for b in range(count)]


def decode(ref, count):
    scales = scales_of(ref, count)
    return [ref[b * BAND:(b + 1) * BAND, :].astype(jnp.int32).astype(F32) * scales[b] for b in range(count)]


def greet(peers):
    barrier = pltpu.get_barrier_semaphore()
    for peer in peers:
        pl.semaphore_signal(barrier, inc=1, device_id=peer, device_id_type=MESH)
    pl.semaphore_wait(barrier, len(peers))


def obs_peers(o):
    z, c = o // 2, o % 2

    def at(step, core):
        return ((z + step + CHIPS) % CHIPS) * 2 + core

    return z, c, at


def remote(src, dst, sems, at, to):
    send, recv = sems
    return pltpu.make_async_remote_copy(
        src_ref=src, dst_ref=dst, send_sem=send.at[at], recv_sem=recv.at[at], device_id=to, device_id_type=MESH,
    )


class Gather:
    def __init__(self, own_ref, out_ref, o, sems, local):
        self.own, self.out, self.o, self.sems = own_ref, out_ref, o, sems
        self.z, self.c, self.at = obs_peers(o)
        self.partner, self.up, self.down = ({"obs": self.at(*p)} for p in ((0, 1 - self.c), (1, self.c), (-1, self.c)))
        self.weeks = own_ref.shape[0]
        self.keep = [pltpu.make_async_copy(own_ref.at[w], out_ref.at[o, w], local.at[w]) for w in range(self.weeks)]
        self.started = []

    def copy(self, role, w, step, core, to):
        ref = self.out.at[self.at(step, core), w]
        return remote(self.own.at[w] if role < 3 else ref, self.out.at[self.o, w] if role < 3 else ref, self.sems, (role, w), to)

    def arrival(self, role, w, step, core):
        ref = self.out.at[self.at(step, core), w]
        remote(self.own.at[w], ref, self.sems, (role, w), self.partner).wait_recv()

    def start(self, *copies):
        for one in copies:
            one.start()
        self.started += copies

    def far_way(self, w):
        return (3, -1, self.up) if w < 2 else (3, 1, self.down)

    def send(self, w):
        self.start(self.copy(1, w, 0, self.c, self.up), self.copy(2, w, 0, self.c, self.down), self.copy(0, w, 0, self.c, self.partner))
        self.keep[w].start()

    def forward(self, w):
        for role, step in ((1, -1), (2, 1)) if w < 2 else ((2, 1), (1, -1)):
            self.arrival(role, w, step, self.c)
            far, far_step, way = self.far_way(w)
            if step == far_step:
                self.start(self.copy(far, w, step, self.c, way))
            self.start(self.copy(3 + role, w, step, self.c, self.partner))

    def relay(self, w):
        self.arrival(3, w, 2, self.c)
        self.start(self.copy(6, w, 2, self.c, self.partner))

    def finish(self):
        for w in range(self.weeks):
            for role, step in ((0, 0), (4, -1), (5, 1), (6, 2)):
                self.arrival(role, w, step, 1 - self.c)
        for one in self.started:
            one.wait_send()
        for one in self.keep:
            one.wait()


def run_gather(gather, order, produce):
    for n, w in enumerate(order):
        produce(w)
        gather.send(w)
        if n >= 1:
            gather.forward(order[n - 1])
        if n >= 2:
            gather.relay(order[n - 2])
    gather.forward(order[-1])
    gather.relay(order[-2])
    gather.relay(order[-1])
    gather.finish()


def halo_copies(src_ref, halo_ref, w, l, bands, sems):
    return [
        remote(src_ref.at[w], halo_ref.at[slot, w], sems, (slot, w), {"lat": (l + step) % bands})
        for slot, step in ((0, 1), (1, bands - 1))
    ]


def stacks_of(low, mid, high):
    return [jnp.concatenate(three, axis=0) for three in zip(low, mid, high)]


def blocks_of(ref, count):
    return [ref[b * BAND:(b + 1) * BAND, :] for b in range(count)]


def put_blocks(ref, blocks):
    for b, value in enumerate(blocks):
        ref[b * BAND:(b + 1) * BAND, :] = value.astype(ref.dtype)


def spread_kernel(sizes, direction_ref, widths_ref, out_ref, field, smooth, wire, halo, shard, send, recv, hsend, hrecv, load, local):
    o, l = lax.axis_index("obs"), lax.axis_index("lat")
    bands, weeks, count, bits, lat_decay, lon_decay = sizes
    loads = [pltpu.make_async_copy(direction_ref.at[o, w], field.at[w], load.at[w]) for w in range(weeks)]
    for one in loads:
        one.start()
    z, c, at = obs_peers(o)
    greet([{"obs": at(0, 1 - c)}, {"obs": at(1, c)}, {"obs": at(-1, c)},
           {"lat": (l + 1) % bands}, {"lat": (l + bands - 1) % bands}])
    lon_width = down_rows(widths_ref[0:1, :])[0:BAND]
    weights = lat_rows(widths_ref, lat_decay, l, bands, False)
    halos = []

    def begin(w):
        loads[w].wait()
        done = along_lon([field[w, :, b * EDGE:(b + 1) * EDGE] for b in range(count)], lon_width, lon_decay, bits)
        encode(wire.at[w], done)
        halos.append(halo_copies(wire, halo, w, l, bands, (hsend, hrecv)))
        for one in halos[w]:
            one.start()
        put_blocks(smooth.at[w], done)

    begin(0)
    begin(1)

    def produce(w):
        if w + 2 < weeks:
            begin(w + 2)
        for one in halos[w]:
            one.wait_recv()
        stacks = stacks_of(decode(halo.at[0, w], count), blocks_of(smooth.at[w], count), decode(halo.at[1, w], count))
        put_blocks(shard.at[w], mix_rows(weights, stacks))

    run_gather(Gather(shard, out_ref, o, (send, recv), local), range(weeks), produce)
    for pair_of in halos:
        for one in pair_of:
            one.wait_send()


def pair(first, second):
    none = jnp.zeros_like(first)
    return jnp.concatenate([jnp.concatenate([first, none], axis=1), jnp.concatenate([none, second], axis=1)], axis=0)


def place_of(col):
    row = (col * 6554) >> 15
    return pl.ds((row >> 5) * WEEK + (col - 5 * row) * BAND + (row & 31), 8, stride=STEP)


def factor_of(scale):
    return (8 >> scale).astype(F32) * 0.125


def forward_kernel(per_step, rows_ref, cols_ref, scale_ref, cells_ref, blocks_ref, out_ref, cells):
    step = pl.program_id(0)

    @pl.when(step == 0)
    def _():
        for k in range(8):
            cells[k * STEP:k * STEP + FIELD, :] = cells_ref[k * FIELD:(k + 1) * FIELD, :].astype(F32)
        out_ref[...] = jnp.zeros_like(out_ref)

    def two(n, carry):
        at = [step * per_step + 2 * n + i for i in range(2)]
        picked = pair(*[cells[place_of(cols_ref[0, 0, a]), :].astype(BF16) for a in at])
        both = jnp.concatenate([blocks_ref[2 * n], blocks_ref[2 * n + 1]], axis=1)
        value = lax.dot_general(picked, both, (((1,), (1,)), ((), ())), preferred_element_type=F32)
        for i, a in enumerate(at):
            row = rows_ref[0, 0, a]
            out_ref[row] = out_ref[row] + value[8 * i:8 * i + 8] * factor_of(scale_ref[0, 0, a])
        return carry

    lax.fori_loop(0, per_step // 2, two, 0, unroll=8)


def adjoint_kernel(per_step, rows_ref, cols_ref, scale_ref, values_ref, blocks_ref, out_ref, total):
    step = pl.program_id(0)

    @pl.when(step == 0)
    def _():
        total[...] = jnp.zeros_like(total)

    def two(n, carry):
        at = [step * per_step + 2 * n + i for i in range(2)]
        pulled = jnp.concatenate([values_ref[rows_ref[0, 0, a]] for a in at], axis=0)
        both = jnp.concatenate([blocks_ref[2 * n], blocks_ref[2 * n + 1]], axis=1)
        value = jnp.dot(pulled, both, preferred_element_type=F32)
        for i, a in enumerate(at):
            place = place_of(cols_ref[0, 0, a])
            part = value[8 * i:8 * i + 8, EDGE * i:EDGE * i + EDGE]
            total[place, :] = total[place, :] + part * factor_of(scale_ref[0, 0, a])
        return carry

    lax.fori_loop(0, per_step // 2, two, 0, unroll=8)

    @pl.when(step == pl.num_programs(0) - 1)
    def _():
        for k in range(8):
            out_ref[k * FIELD:(k + 1) * FIELD, :] = total[k * STEP:k * STEP + FIELD, :]


def sum_bands_kernel(bands, part_ref, weight_ref, out_ref, got, shard, send, recv, send2, recv2):
    l = lax.axis_index("lat")
    share = part_ref.shape[0] // bands
    greet([{"lat": (l + d) % bands} for d in range(1, bands)])
    mine = pl.ds(l * share, share)

    def first(d):
        peer = (l + d) % bands
        return pltpu.make_async_remote_copy(
            src_ref=part_ref.at[pl.ds(peer * share, share)], dst_ref=got.at[d], send_sem=send.at[d], recv_sem=recv.at[d],
            device_id={"lat": peer}, device_id_type=MESH,
        )

    def second(d, owner):
        return pltpu.make_async_remote_copy(
            src_ref=shard, dst_ref=out_ref.at[pl.ds(owner * share, share)], send_sem=send2.at[d], recv_sem=recv2.at[d],
            device_id={"lat": (l + d) % bands}, device_id_type=MESH,
        )

    for d in range(1, bands):
        first(d).start()
    total = part_ref[mine]
    for d in range(1, bands):
        first(d).wait_recv()
        total = total + got[d]
    weight = weight_ref[mine]
    shard[...] = (total * weight).astype(shard.dtype)
    for d in range(1, bands):
        second(d, l).start()
    out_ref[mine] = shard[...]
    for d in range(1, bands):
        second(d, (l + bands - d) % bands).wait_recv()
    for d in range(1, bands):
        first(d).wait_send()
        second(d, l).wait_send()


def image_kernel(sizes, part_ref, widths_ref, out_ref, own, there, far_out, near_out, relay_out, far_in, near_in, relay_in,
                 mine, band, halo, shard, send, recv, hsend, hrecv, psend, precv, rsend, rrecv, load, local):
    o, l = lax.axis_index("obs"), lax.axis_index("lat")
    bands, weeks, count, bits, lat_decay, lon_decay = sizes
    z, c, at = obs_peers(o)
    partner, up, down = {"obs": at(0, 1 - c)}, {"obs": at(1, c)}, {"obs": at(-1, c)}
    greet([partner, up, down, {"lat": (l + 1) % bands}, {"lat": (l + bands - 1) % bands}])
    order = (0, 2, 1, 3)

    def rows_for(core, w):
        return part_ref.at[:, core, w]

    swaps = [remote(rows_for(1 - c, w), there.at[w], (psend, precv), w, partner) for w in range(weeks)]
    loads = [pltpu.make_async_copy(rows_for(c, w), own.at[w], load.at[w]) for w in range(weeks)]
    for w in order:
        swaps[w].start()
        loads[w].start()
    lon_width = down_rows(widths_ref[0:1, :])[0:BAND]
    weights = lat_rows(widths_ref, lat_decay, l, bands, True)
    ring = (rsend, rrecv)

    def way(w):
        return (1, up, down) if w < 2 else (-1, down, up)

    far = [remote(far_out.at[w], far_in.at[w], ring, (0, w), way(w)[1]) for w in range(weeks)]
    relayed = [remote(relay_out.at[w], relay_in.at[w], ring, (1, w), way(w)[1]) for w in range(weeks)]
    near = [remote(near_out.at[w], near_in.at[w], ring, (2, w), way(w)[2]) for w in range(weeks)]
    halos = [halo_copies(band, halo, w, l, bands, (hsend, hrecv)) for w in range(weeks)]

    def chip_sum(w, step):
        there_too = (z + step + CHIPS) % CHIPS
        return [x + y for x, y in zip(blocks_of(own.at[w, there_too], count), blocks_of(there.at[w, there_too], count))]

    def plus(x, y):
        return [a + d for a, d in zip(x, y)]

    for w in order:
        swaps[w].wait_recv()
        loads[w].wait()
        encode(far_out.at[w], chip_sum(w, 2))
        far[w].start()
        encode(near_out.at[w], chip_sum(w, -way(w)[0]))
        near[w].start()
    for w in order:
        far[w].wait_recv()
        encode(relay_out.at[w], plus(chip_sum(w, way(w)[0]), decode(far_in.at[w], count)))
        relayed[w].start()
    for w in order:
        near[w].wait_recv()
        relayed[w].wait_recv()
        total = plus(plus(chip_sum(w, 0), decode(near_in.at[w], count)), decode(relay_in.at[w], count))
        encode(band.at[w], total)
        for one in halos[w]:
            one.start()
        put_blocks(mine.at[w], total)

    def produce(w):
        for one in halos[w]:
            one.wait_recv()
        stacks = stacks_of(decode(halo.at[0, w], count), blocks_of(mine.at[w], count), decode(halo.at[1, w], count))
        encode(shard.at[w], along_lon(mix_rows(weights, stacks), lon_width, lon_decay, bits))

    run_gather(Gather(shard, out_ref, o, (send, recv), local), order, produce)
    for w in range(weeks):
        for one in (swaps[w], far[w], relayed[w], near[w], *halos[w]):
            one.wait_send()


def change_block(change_ref, i, b, first, rows):
    at = b * BAND + first
    at = at if isinstance(at, int) else pl.multiple_of(at, 16)
    power = change_ref[i, 0, WEEK:CODED, :].astype(jnp.int32).astype(F32)
    pick = jnp.sum(jnp.where(iota((16, EDGE), 0) == b, power, 0.0), axis=0, keepdims=True)
    return change_ref[i, 0, pl.ds(at, rows), :].astype(jnp.int32).astype(F32) * (jnp.exp2(pick) * (1.0 / TOP))


def gram_kernel(k, residual_ref, direction_ref, change_ref, out_ref, sums):
    step = pl.program_id(0)
    lon_blocks = 5

    @pl.when(step == 0)
    def _():
        sums[...] = jnp.zeros_like(sums)

    def one(b, carry):
        lanes = pl.ds(pl.multiple_of(b * EDGE, EDGE), EDGE)
        res = [residual_ref[i, 0, :, lanes] for i in range(k)]
        dire = [direction_ref[i, 0, :, lanes] for i in range(k)]
        img = [dire[i] + change_block(change_ref, i, b, 0, BAND) for i in range(k)]

        def add(t, i, j, x, y):
            sums[t, i, j] = sums[t, i, j] + jnp.sum((x * y).reshape(4, 8, EDGE), axis=0)

        for i in range(k):
            for j in range(k):
                if i <= j:
                    add(0, i, j, res[i], res[j])
                    add(3, i, j, img[i], img[j])
                add(1, i, j, dire[i], img[j])
                add(2, i, j, img[i], res[j])
        return carry

    lax.fori_loop(0, lon_blocks, one, 0)

    @pl.when(step == pl.num_programs(0) - 1)
    def _():
        lane, row = iota((k, EDGE), 1), iota((k, EDGE), 0)
        result = jnp.zeros((k, EDGE), F32)
        for t in range(4):
            for i in range(k):
                line = jnp.sum(jnp.sum(sums[t, i], axis=1), axis=1, keepdims=True)
                line = jnp.broadcast_to(line, (k, EDGE))
                result = jnp.where(lane == t * k + i, line, result)
        out_ref[...] = result


def flip(x):
    square = jnp.concatenate([x, jnp.zeros((EDGE - 8, EDGE), F32)], axis=0)
    return jnp.transpose(square)[:8, :]


def product(x, y):
    return sum(jnp.broadcast_to(x[:, i:i + 1], (8, EDGE)) * jnp.broadcast_to(y[i:i + 1, :], (8, EDGE)) for i in range(8))


def solve(a, b):
    row = iota((8, EDGE), 0)
    for p in range(8):
        line = jnp.broadcast_to(a[p:p + 1, :], (8, EDGE))
        line_b = jnp.broadcast_to(b[p:p + 1, :], (8, EDGE))
        column = jnp.broadcast_to(a[:, p:p + 1], (8, EDGE))
        inverse = 1.0 / jnp.broadcast_to(a[p:p + 1, p:p + 1], (8, EDGE))
        ratio = column * inverse
        here = row == p
        a = jnp.where(here, line * inverse, a - ratio * line)
        b = jnp.where(here, line_b * inverse, b - ratio * line_b)
    return b


def solve_kernel(bands, part_ref, out_ref, got, send, recv):
    l = lax.axis_index("lat")
    greet([{"lat": (l + d) % bands} for d in range(1, bands)])

    def to(d):
        return pltpu.make_async_remote_copy(
            src_ref=part_ref, dst_ref=got.at[l], send_sem=send.at[d], recv_sem=recv.at[d],
            device_id={"lat": (l + d) % bands}, device_id_type=MESH,
        )

    for d in range(1, bands):
        to(d).start()
    got[l] = part_ref[...]
    for d in range(1, bands):
        to(d).wait_recv()
    total = got[0]
    for d in range(1, bands):
        total = total + got[d]
    lane, row = iota((8, EDGE), 1), iota((8, EDGE), 0)
    parts = []
    for t in range(4):
        moved = total if t == 0 else pltpu.roll(total, EDGE - 8 * t, 1)
        parts.append(jnp.where(lane < 8, moved, 0.0))

    def full(x):
        low = jnp.where(lane <= row, x, 0.0)
        return low + flip(jnp.where(lane < row, x, 0.0))

    gram_old, image_image = full(parts[0]), full(parts[3])
    curvature = 0.5 * (parts[1] + flip(parts[1]))
    residual_image = parts[2]
    step = solve(curvature, gram_old)
    cross = product(residual_image, step)
    gram_new = gram_old - cross - flip(cross) + product(flip(step), product(image_image, step))
    turn = solve(gram_old, gram_new)
    out_ref[...] = jnp.where(lane < 8, step, 0.0) + pltpu.roll(jnp.where(lane < 8, turn, 0.0), 8, 1)
    for d in range(1, bands):
        to(d).wait_send()


def update_kernel(k, coef_ref, solution_ref, residual_ref, direction_ref, change_ref, sol_out, res_out, dir_out):
    rows_each = 32

    def one(b, carry):
        lanes = pl.ds(pl.multiple_of(b * EDGE, EDGE), EDGE)
        for r in range(BAND // rows_each):
            rows = slice(r * rows_each, (r + 1) * rows_each)
            dire = [direction_ref[i, 0, rows, lanes] for i in range(k)]
            more = [change_block(change_ref, i, b, r * rows_each, rows_each) for i in range(k)]
            for a in range(k):
                forth = sum(coef_ref[i, a] * dire[i] for i in range(k))
                back = sum(coef_ref[i, a] * more[i] for i in range(k))
                turn = sum(coef_ref[i, k + a] * dire[i] for i in range(k))
                left = residual_ref[a, 0, rows, lanes] - (forth + back)
                sol_out[a, 0, rows, lanes] = solution_ref[a, 0, rows, lanes] + forth
                res_out[a, 0, rows, lanes] = left
                dir_out[a, 0, rows, lanes] = left + turn
        return carry

    lax.fori_loop(0, 5, one, 0)


def params(collective=None, limit=None):
    extra = {} if collective is None else {"collective_id": collective, "has_side_effects": True}
    return pltpu.CompilerParams(vmem_limit_bytes=limit or (48 << 20), **extra)


def shards(bands, footprints, block_rows, block_cols, block_scale, lat_width, lon_width, obs_weight, solution, residual, direction):
    k, weeks, band_rows, nlon = direction.shape
    blocks = footprints.shape[2]
    count = nlon // EDGE
    assert (k, weeks, band_rows, count) == (8, 4, BAND, 5)
    row_blocks = obs_weight.shape[0] // EDGE
    sizes = (bands, weeks, count, (nlon // 8 + 1).bit_length(), band_rows / 2.0, nlon / 32.0)
    l = lax.axis_index("lat")
    lon_own = lax.dynamic_slice_in_dim(lon_width, l * BAND, BAND)
    lat_near = lax.dynamic_slice_in_dim(jnp.pad(lat_width, BAND), l * BAND, 3 * BAND)
    widths = jnp.pad(jnp.stack([jnp.pad(lon_own, (0, 3 * BAND)), jnp.pad(lat_near, (0, BAND))]), ((0, 6), (0, 0))).astype(F32)
    all_rows = k * weeks * WEEK
    plain, coded = (weeks, WEEK, EDGE), (weeks, CODED, EDGE)
    ints = jnp.int16

    cells = pl.pallas_call(
        functools.partial(spread_kernel, sizes),
        out_shape=jax.ShapeDtypeStruct((k, *plain), BF16),
        in_specs=[ANY_SPEC, VMEM_SPEC],
        out_specs=ANY_SPEC,
        scratch_shapes=[
            VMEM((weeks, band_rows, nlon), F32), VMEM(plain, F32), VMEM(coded, ints), VMEM((2, *coded), ints), VMEM(plain, BF16),
            DMA((7, weeks)), DMA((7, weeks)), DMA((2, weeks)), DMA((2, weeks)), DMA((weeks,)), DMA((weeks,)),
        ],
        compiler_params=params(1, 65_000_000),
        name="spread",
    )(direction, widths)

    per_step = 48
    smem = [SMEM_SPEC] * 3
    block_spec = pl.BlockSpec((None, None, per_step, EDGE, EDGE), lambda i: (0, 0, i, 0, 0))
    forward = pl.pallas_call(
        functools.partial(forward_kernel, per_step),
        grid=(blocks // per_step,),
        out_shape=jax.ShapeDtypeStruct((row_blocks, k, EDGE), F32),
        in_specs=smem + [pl.BlockSpec((all_rows, EDGE), lambda i: (0, 0)), block_spec],
        out_specs=pl.BlockSpec((row_blocks, k, EDGE), lambda i: (0, 0, 0)),
        scratch_shapes=[VMEM((k * STEP, EDGE), F32)],
        compiler_params=params(),
        name="forward",
    )(block_rows, block_cols, block_scale, cells.reshape(all_rows, EDGE), footprints)

    share = row_blocks // bands
    values = pl.pallas_call(
        functools.partial(sum_bands_kernel, bands),
        out_shape=jax.ShapeDtypeStruct((row_blocks, k, EDGE), BF16),
        in_specs=[VMEM_SPEC, VMEM_SPEC],
        out_specs=VMEM_SPEC,
        scratch_shapes=[
            VMEM((bands, share, k, EDGE), F32), VMEM((share, k, EDGE), BF16),
            DMA((bands,)), DMA((bands,)), DMA((bands,)), DMA((bands,)),
        ],
        compiler_params=params(2),
        name="sum_bands",
    )(forward, obs_weight.reshape(row_blocks, 1, EDGE))

    part = pl.pallas_call(
        functools.partial(adjoint_kernel, per_step),
        grid=(blocks // per_step,),
        out_shape=jax.ShapeDtypeStruct((all_rows, EDGE), F32),
        in_specs=smem + [pl.BlockSpec((row_blocks, k, EDGE), lambda i: (0, 0, 0)), block_spec],
        out_specs=pl.BlockSpec((all_rows, EDGE), lambda i: (0, 0)),
        scratch_shapes=[VMEM((k * STEP, EDGE), F32)],
        compiler_params=params(),
        name="adjoint",
    )(block_rows, block_cols, block_scale, values, footprints)

    change = pl.pallas_call(
        functools.partial(image_kernel, sizes),
        out_shape=jax.ShapeDtypeStruct((k, *coded), ints),
        in_specs=[ANY_SPEC, VMEM_SPEC],
        out_specs=ANY_SPEC,
        scratch_shapes=[
            VMEM((weeks, CHIPS, WEEK, EDGE), F32), VMEM((weeks, CHIPS, WEEK, EDGE), F32),
            *[VMEM(coded, ints)] * 6, VMEM(plain, F32), VMEM(coded, ints), VMEM((2, *coded), ints), VMEM(coded, ints),
            DMA((7, weeks)), DMA((7, weeks)), DMA((2, weeks)), DMA((2, weeks)), DMA((weeks,)), DMA((weeks,)),
            DMA((3, weeks)), DMA((3, weeks)), DMA((weeks,)), DMA((weeks,)),
        ],
        compiler_params=params(3),
        name="image",
    )(part.reshape(CHIPS, 2, *plain), widths)

    native = pl.BlockSpec((k, 1, band_rows, nlon), lambda w: (0, w, 0, 0))
    packed = pl.BlockSpec((k, 1, CODED, EDGE), lambda w: (0, w, 0, 0))
    gram = pl.pallas_call(
        functools.partial(gram_kernel, k),
        grid=(weeks,),
        out_shape=jax.ShapeDtypeStruct((k, EDGE), F32),
        in_specs=[native, native, packed],
        out_specs=pl.BlockSpec((k, EDGE), lambda w: (0, 0)),
        scratch_shapes=[VMEM((4, k, k, 8, EDGE), F32)],
        compiler_params=params(),
        name="gram",
    )(residual, direction, change)

    coef = pl.pallas_call(
        functools.partial(solve_kernel, bands),
        out_shape=jax.ShapeDtypeStruct((k, EDGE), F32),
        in_specs=[VMEM_SPEC],
        out_specs=VMEM_SPEC,
        scratch_shapes=[VMEM((bands, k, EDGE), F32), DMA((bands,)), DMA((bands,))],
        compiler_params=params(4),
        name="solve",
    )(gram)

    return pl.pallas_call(
        functools.partial(update_kernel, k),
        grid=(weeks,),
        out_shape=[jax.ShapeDtypeStruct(direction.shape, F32)] * 3,
        in_specs=[SMEM_SPEC, native, native, native, packed],
        out_specs=[native] * 3,
        compiler_params=params(),
        name="update",
    )(coef, solution, residual, direction, change)


def solution(mesh):
    assert mesh.shape["obs"] == 2 * CHIPS
    three = (P(None, None, "lat", None),) * 3
    blocks = P("obs", "lat", None)
    return jax.shard_map(
        functools.partial(shards, mesh.shape["lat"]),
        mesh=mesh,
        in_specs=(P("obs", "lat", None, None, None), blocks, blocks, blocks, P(), P(), P("obs"), *three),
        out_specs=three,
        check_vma=False,
    )
```

time: 156 us -> 127 us (0.81)
  Pallas kernels: 147 us -> 122 us
  local copies, waits for them, and re-layouts: 4.88 us -> 2.88 us
    pallas_call x1, Pallas kernels: 48.5 us -> 34.3 us  [shards(): pl.pallas_call(functools.partial(image_kernel, sizes), out_shape=jax.Shap...]
    pallas_call x1, Pallas kernels: 14 us -> 10.1 us  [shards(): pl.pallas_call(functools.partial(forward_kernel, per_step), grid=(blocks...]
    pallas_call x1, Pallas kernels: 12.9 us -> 9.53 us  [shards(): pl.pallas_call(functools.partial(adjoint_kernel, per_step), grid=(blocks...]
    unnamed x3 -> x0, other arithmetic: 2.1 us -> none
    unnamed x12 -> x16, local copies, waits for them, and re-layouts: 3.26 us -> 1.34 us
    pallas_call x1, Pallas kernels: 14.8 us -> 13.1 us  [shards(): pl.pallas_call(functools.partial(sum_bands_kernel, bands), out_shape=jax....]
    pallas_call x1, Pallas kernels: 30.5 us -> 28.8 us  [shards(): pl.pallas_call(functools.partial(spread_kernel, sizes), out_shape=jax.Sha...]
where the time goes in v2:
time: 127 us; the launch traced here: 126 us
  Pallas kernels  122 us (96%)
  local copies, waits for them, and re-layouts  2.88 us (2%)
    pallas_call x1, Pallas kernels, shards(): pl.pallas_call(functools.partial(image_kernel, sizes), out_shape=jax.Shap...  34.3 us
    pallas_call x1, Pallas kernels, shards(): pl.pallas_call(functools.partial(spread_kernel, sizes), out_shape=jax.Sha...  28.8 us
    pallas_call x1, Pallas kernels, shards(): pl.pallas_call(functools.partial(sum_bands_kernel, bands), out_shape=jax....  13.1 us
    pallas_call x1, Pallas kernels, shards(): pl.pallas_call(functools.partial(forward_kernel, per_step), grid=(blocks...  10.1 us
    pallas_call x1, Pallas kernels, shards(): pl.pallas_call(functools.partial(solve_kernel, bands), out_shape=jax.Shap...  10.1 us
    pallas_call x1, Pallas kernels, shards(): pl.pallas_call(functools.partial(adjoint_kernel, per_step), grid=(blocks...  9.53 us
    pallas_call x1, Pallas kernels, shards(): pl.pallas_call(functools.partial(update_kernel, k), grid=(weeks,), out_sh...  8.88 us
    pallas_call x1, Pallas kernels, shards(): pl.pallas_call(functools.partial(gram_kernel, k), grid=(weeks,), out_shap...  7.15 us

profile of v2, /device:TPU:0, one launch (start us, length us, event | category | flops | bytes accessed | tf_op | source)
XLA Modules:
  0.0 126.3 jit_solution(10857406457695987236)
XLA Ops:
  0.6 0.0 copy-start.7
  0.6 0.0 copy-start.6
  0.7 0.0 copy-start.5
  0.7 0.8 dynamic_slice.6
  1.4 0.8 pad_dynamic-slice_fusion
  2.2 0.6 pad_convert_fusion.widths_ref
  2.8 28.8 %spread.1 = bf16[8,4,160,128]{3,2,1,0:T(8,128)(2,1)} custom-call(f32[8,4,32,640]{3,2,1,0:T(8,128)} %direction_ref.5, f32[8,128]{1,0:T(8,128)} %pad_convert_fusion.widths_ref), custom_call_target="tpu_custom_call" | custom-call | tf_op jit(solution)/shard_map/spread/pallas_call | solution.py:582
  31.6 0.0 copy-done.7
  31.6 0.0 copy-done.6
  31.6 0.0 copy-done.5
  31.6 0.0 copy-start.1
  31.6 1.3 %copy-done.1 = bf16[8,4,160,128]{3,2,1,0:T(8,128)(2,1)S(1)} copy-done((bf16[8,4,160,128]{3,2,1,0:T(8,128)(2,1)S(1)}, bf16[8,4,160,128]{3,2,1,0:T(8,128)(2,1)}, u32[]{:S(2)}) %copy-start.1) | copy-done | bytes 1310744
  32.9 0.0 copy-start.4
  32.9 10.1 %forward.1.part_ref = f32[32,8,128]{2,1,0:T(8,128)S(1)} custom-call(s32[1,1,384]{2,1,0:T(1,128)S(1)} %copy-done.5, s32[1,1,384]{2,1,0:T(1,128)S(1)} %copy-done.6, s32[1,1,384]{2,1,0:T(1,128)S(1)} %copy-done.7, bf16[5120,128]{1,0:T(8,128)(2,1)S(1)} %bitcast.8, bf16[1,1,384,128,128]{4,3,2,1,0:T(8,128)(2,1)} %blocks_ref.3), custom_call_target="tpu_custom_call" | custom-call | tf_op jit(solution)/shard_map/forward/pallas_call | solution.py:598
  43.1 0.0 copy-done.4
  43.1 13.1 %sum_bands.1.values_ref = bf16[32,8,128]{2,1,0:T(8,128)(2,1)S(1)} custom-call(f32[32,8,128]{2,1,0:T(8,128)S(1)} %forward.1.part_ref, f32[32,1,128]{2,1,0:T(1,128)S(1)} %bitcast.9), custom_call_target="tpu_custom_call" | custom-call | tf_op jit(solution)/shard_map/sum_bands/pallas_call | solution.py:610
  56.2 0.0 copy-start.3
  56.2 9.5 %adjoint.1 = f32[5120,128]{1,0:T(8,128)S(1)} custom-call(s32[1,1,384]{2,1,0:T(1,128)S(1)} %copy-done.5, s32[1,1,384]{2,1,0:T(1,128)S(1)} %copy-done.6, s32[1,1,384]{2,1,0:T(1,128)S(1)} %copy-done.7, bf16[32,8,128]{2,1,0:T(8,128)(2,1)S(1)} %sum_bands.1.values_ref, bf16[1,1,384,128,128]{4,3,2,1,0:T(8,128)(2,1)} %blocks_ref.3), custom_call_target="tpu_custom_call" | custom-call | tf_op jit(solution)/shard_map/adjoint/pallas_call | solution.py:623
  65.7 0.0 copy-start
  65.7 0.0 copy-done.3
  65.8 34.3 %image.1.change_ref = s16[8,4,176,128]{3,2,1,0:T(8,128)(2,1)S(1)} custom-call(f32[4,2,4,160,128]{4,3,2,1,0:T(8,128)S(1)} %bitcast.7, f32[8,128]{1,0:T(8,128)S(1)} %copy-done.3), custom_call_target="tpu_custom_call" | custom-call | tf_op jit(solution)/shard_map/image/pallas_call | solution.py:634
  100.1 0.0 copy-done
  100.1 0.0 copy-start.2
  100.1 7.1 %gram.1.part_ref = f32[8,128]{1,0:T(8,128)S(1)} custom-call(f32[8,4,32,640]{3,2,1,0:T(8,128)S(1)} %copy-done, f32[8,4,32,640]{3,2,1,0:T(8,128)} %direction_ref.5, s16[8,4,176,128]{3,2,1,0:T(8,128)(2,1)S(1)} %image.1.change_ref), custom_call_target="tpu_custom_call" | custom-call | tf_op jit(solution)/shard_map/gram/pallas_call | solution.py:651
  107.2 10.1 %solve.1.coef_ref = f32[8,128]{1,0:T(8,128)S(1)} custom-call(f32[8,128]{1,0:T(8,128)S(1)} %gram.1.part_ref), custom_call_target="tpu_custom_call" | custom-call | tf_op jit(solution)/shard_map/solve/pallas_call | solution.py:662
  117.4 0.0 copy-done.2
  117.4 8.9 %update.1 = (f32[8,4,32,640]{3,2,1,0:T(8,128)}, f32[8,4,32,640]{3,2,1,0:T(8,128)}, f32[8,4,32,640]{3,2,1,0:T(8,128)}) custom-call(f32[8,128]{1,0:T(8,128)S(1)} %solve.1.coef_ref, f32[8,4,32,640]{3,2,1,0:T(8,128)S(1)} %copy-done.2, f32[8,4,32,640]{3,2,1,0:T(8,128)} %residual_ref.3, f32[8,4,32,640]{3,2,1,0:T(8,128)} %direction_ref.5, ...), custom_call_target="tpu_custom_call" | custom-call | tf_op jit(solution)/shard_map/update/pallas_call | solution.py:672
  (2 shorter events, 0.0 us)
Async XLA Ops:
  0.6 30.9 %copy-start.7 = (s32[1,1,384]{2,1,0:T(1,128)S(1)}, s32[1,1,384]{2,1,0:T(1,128)}, u32[]{:S(2)}) copy-start(s32[1,1,384]{2,1,0:T(1,128)} %scale_ref.3) | copy-start | bytes 4612
  0.6 30.9 %copy-start.6 = (s32[1,1,384]{2,1,0:T(1,128)S(1)}, s32[1,1,384]{2,1,0:T(1,128)}, u32[]{:S(2)}) copy-start(s32[1,1,384]{2,1,0:T(1,128)} %cols_ref.3) | copy-start | bytes 4612
  0.7 30.9 %copy-start.5 = (s32[1,1,384]{2,1,0:T(1,128)S(1)}, s32[1,1,384]{2,1,0:T(1,128)}, u32[]{:S(2)}) copy-start(s32[1,1,384]{2,1,0:T(1,128)} %rows_ref.3) | copy-start | bytes 4612
  31.6 1.3 %copy-start.1 = (bf16[8,4,160,128]{3,2,1,0:T(8,128)(2,1)S(1)}, bf16[8,4,160,128]{3,2,1,0:T(8,128)(2,1)}, u32[]{:S(2)}) copy-start(bf16[8,4,160,128]{3,2,1,0:T(8,128)(2,1)} %spread.1) | copy-start | bytes 3932164
  32.9 10.2 %copy-start.4 = (f32[4096]{0:T(1024)S(1)}, f32[4096]{0:T(1024)}, u32[]{:S(2)}) copy-start(f32[4096]{0:T(1024)} %param.16) | copy-start | bytes 49156
  56.2 9.6 %copy-start.3 = (f32[8,128]{1,0:T(8,128)S(1)}, f32[8,128]{1,0:T(8,128)}, u32[]{:S(2)}) copy-start(f32[8,128]{1,0:T(8,128)} %pad_convert_fusion.widths_ref) | copy-start | bytes 12292
  65.7 34.3 %copy-start = (f32[8,4,32,640]{3,2,1,0:T(8,128)S(1)}, f32[8,4,32,640]{3,2,1,0:T(8,128)}, u32[]{:S(2)}) copy-start(f32[8,4,32,640]{3,2,1,0:T(8,128)} %residual_ref.3) | copy-start | bytes 7864324
  100.1 17.3 %copy-start.2 = (f32[8,4,32,640]{3,2,1,0:T(8,128)S(1)}, f32[8,4,32,640]{3,2,1,0:T(8,128)}, u32[]{:S(2)}) copy-start(f32[8,4,32,640]{3,2,1,0:T(8,128)} %solution_ref.1) | copy-start | bytes 7864324

commit v3 on v2

--- a/solution.py
+++ b/solution.py
@@ -176,17 +176,17 @@
         self.arrival(3, w, 2, self.c)
         self.start(self.copy(6, w, 2, self.c, self.partner))
 
+    def complete(self, w):
+        for role, step in ((0, 0), (4, -1), (5, 1), (6, 2)):
+            self.arrival(role, w, step, 1 - self.c)
+        self.keep[w].wait()
+
     def finish(self):
-        for w in range(self.weeks):
-            for role, step in ((0, 0), (4, -1), (5, 1), (6, 2)):
-                self.arrival(role, w, step, 1 - self.c)
         for one in self.started:
             one.wait_send()
-        for one in self.keep:
-            one.wait()
-
-
-def run_gather(gather, order, produce):
+
+
+def run_gather(gather, order, produce, consume):
     for n, w in enumerate(order):
         produce(w)
         gather.send(w)
@@ -194,9 +194,17 @@
             gather.forward(order[n - 1])
         if n >= 2:
             gather.relay(order[n - 2])
+        if n >= 3:
+            gather.complete(order[n - 3])
+            consume(order[n - 3])
     gather.forward(order[-1])
     gather.relay(order[-2])
+    gather.complete(order[-3])
+    consume(order[-3])
     gather.relay(order[-1])
+    for w in order[-2:]:
+        gather.complete(w)
+        consume(w)
     gather.finish()
 
 
@@ -253,7 +261,7 @@
         stacks = stacks_of(decode(halo.at[0, w], count), blocks_of(smooth.at[w], count), decode(halo.at[1, w], count))
         put_blocks(shard.at[w], mix_rows(weights, stacks))
 
-    run_gather(Gather(shard, out_ref, o, (send, recv), local), range(weeks), produce)
+    run_gather(Gather(shard, out_ref, o, (send, recv), local), range(weeks), produce, lambda w: None)
     for pair_of in halos:
         for one in pair_of:
             one.wait_send()
@@ -358,13 +366,18 @@
         second(d, l).wait_send()
 
 
-def image_kernel(sizes, part_ref, widths_ref, out_ref, own, there, far_out, near_out, relay_out, far_in, near_in, relay_in,
-                 mine, band, halo, shard, send, recv, hsend, hrecv, psend, precv, rsend, rrecv, load, local):
+def image_kernel(sizes, part_ref, widths_ref, residual_ref, direction_ref, out_ref, coef_ref, own, there, far_out, near_out,
+                 relay_out, far_in, near_in, relay_in, mine, band, halo, shard, everyone, res, dire, sums, line_got, line_sum,
+                 send, recv, hsend, hrecv, psend, precv, rsend, rrecv, lsend, lrecv, load, local, fields, leave):
     o, l = lax.axis_index("obs"), lax.axis_index("lat")
     bands, weeks, count, bits, lat_decay, lon_decay = sizes
     z, c, at = obs_peers(o)
     partner, up, down = {"obs": at(0, 1 - c)}, {"obs": at(1, c)}, {"obs": at(-1, c)}
-    greet([partner, up, down, {"lat": (l + 1) % bands}, {"lat": (l + bands - 1) % bands}])
+    k, side = 2 * CHIPS, CHIPS
+    x, y = l // side, l % side
+    lines = [[{"lat": x * side + (y + d) % side} for d in range(1, side)], [{"lat": (x + d) % side * side + y} for d in range(1, side)]]
+    gets = [pltpu.make_async_copy(residual_ref, res, fields.at[0]), pltpu.make_async_copy(direction_ref, dire, fields.at[1])]
+    greet([partner, up, down, {"lat": (l + 1) % bands}, {"lat": (l + bands - 1) % bands}, *lines[0], *lines[1]])
     order = (0, 2, 1, 3)
 
     def rows_for(core, w):
@@ -375,6 +388,9 @@
     for w in order:
         swaps[w].start()
         loads[w].start()
+    for one in gets:
+        one.start()
+    sums[...] = jnp.zeros_like(sums)
     lon_width = down_rows(widths_ref[0:1, :])[0:BAND]
     weights = lat_rows(widths_ref, lat_decay, l, bands, True)
     ring = (rsend, rrecv)
@@ -401,11 +417,18 @@
         far[w].start()
         encode(near_out.at[w], chip_sum(w, -way(w)[0]))
         near[w].start()
+    gets[0].wait()
+    for w in (0, 1):
+        gram_first(k, count, w, res, sums)
     for w in order:
         far[w].wait_recv()
         encode(relay_out.at[w], plus(chip_sum(w, way(w)[0]), decode(far_in.at[w], count)))
         relayed[w].start()
     for w in order:
+        if w == order[0]:
+            for early in (2, 3):
+                gram_first(k, count, early, res, sums)
+            gets[1].wait()
         near[w].wait_recv()
         relayed[w].wait_recv()
         total = plus(plus(chip_sum(w, 0), decode(near_in.at[w], count)), decode(relay_in.at[w], count))
@@ -420,58 +443,84 @@
         stacks = stacks_of(decode(halo.at[0, w], count), blocks_of(mine.at[w], count), decode(halo.at[1, w], count))
         encode(shard.at[w], along_lon(mix_rows(weights, stacks), lon_width, lon_decay, bits))
 
-    run_gather(Gather(shard, out_ref, o, (send, recv), local), order, produce)
+    leaving = [pltpu.make_async_copy(everyone.at[:, w], out_ref.at[:, w], leave.at[w]) for w in range(weeks)]
+
+    def consume(w):
+        leaving[w].start()
+        gram_week(k, count, w, res, dire, everyone, sums)
+
+    run_gather(Gather(shard, everyone, o, (send, recv), local), order, produce, consume)
+    total = gram_total(k, sums)
+    for axis, here in ((0, y), (1, x)):
+        line_sum[axis] = total
+        copies = [remote(line_sum.at[axis], line_got.at[axis, here], (lsend, lrecv), (axis, d), to) for d, to in enumerate(lines[axis])]
+        for one in copies:
+            one.start()
+        line_got[axis, here] = total
+        for d in range(side - 1):
+            back = (here + side - 1 - d) % side
+            remote(line_sum.at[axis], line_got.at[axis, back], (lsend, lrecv), (axis, d), lines[axis][d]).wait_recv()
+        total = line_got[axis, 0] + line_got[axis, 1] + line_got[axis, 2] + line_got[axis, 3]
+        for one in copies:
+            one.wait_send()
+    coef_ref[...] = coefficients(total)
     for w in range(weeks):
+        leaving[w].wait()
         for one in (swaps[w], far[w], relayed[w], near[w], *halos[w]):
             one.wait_send()
 
 
-def change_block(change_ref, i, b, first, rows):
+def change_block(change_ref, i, w, b, first, rows):
     at = b * BAND + first
     at = at if isinstance(at, int) else pl.multiple_of(at, 16)
-    power = change_ref[i, 0, WEEK:CODED, :].astype(jnp.int32).astype(F32)
+    power = change_ref[i, w, WEEK:CODED, :].astype(jnp.int32).astype(F32)
     pick = jnp.sum(jnp.where(iota((16, EDGE), 0) == b, power, 0.0), axis=0, keepdims=True)
-    return change_ref[i, 0, pl.ds(at, rows), :].astype(jnp.int32).astype(F32) * (jnp.exp2(pick) * (1.0 / TOP))
-
-
-def gram_kernel(k, residual_ref, direction_ref, change_ref, out_ref, sums):
-    step = pl.program_id(0)
-    lon_blocks = 5
-
-    @pl.when(step == 0)
-    def _():
-        sums[...] = jnp.zeros_like(sums)
-
+    return change_ref[i, w, pl.ds(at, rows), :].astype(jnp.int32).astype(F32) * (jnp.exp2(pick) * (1.0 / TOP))
+
+
+def add_gram(sums, t, i, j, x, y):
+    sums[t, i, j] = sums[t, i, j] + jnp.sum((x * y).reshape(BAND // 8, 8, EDGE), axis=0)
+
+
+def lanes_of(b):
+    return pl.ds(pl.multiple_of(b * EDGE, EDGE), EDGE)
+
+
+def gram_first(k, count, w, res_ref, sums):
     def one(b, carry):
-        lanes = pl.ds(pl.multiple_of(b * EDGE, EDGE), EDGE)
-        res = [residual_ref[i, 0, :, lanes] for i in range(k)]
-        dire = [direction_ref[i, 0, :, lanes] for i in range(k)]
-        img = [dire[i] + change_block(change_ref, i, b, 0, BAND) for i in range(k)]
-
-        def add(t, i, j, x, y):
-            sums[t, i, j] = sums[t, i, j] + jnp.sum((x * y).reshape(4, 8, EDGE), axis=0)
-
+        res = [res_ref[i, w, :, lanes_of(b)] for i in range(k)]
+        for i in range(k):
+            for j in range(i, k):
+                add_gram(sums, 0, i, j, res[i], res[j])
+        return carry
+
+    lax.fori_loop(0, count, one, 0)
+
+
+def gram_week(k, count, w, res_ref, dire_ref, change_ref, sums):
+    def one(b, carry):
+        res = [res_ref[i, w, :, lanes_of(b)] for i in range(k)]
+        dire = [dire_ref[i, w, :, lanes_of(b)] for i in range(k)]
+        img = [dire[i] + change_block(change_ref, i, w, b, 0, BAND) for i in range(k)]
         for i in range(k):
             for j in range(k):
                 if i <= j:
-                    add(0, i, j, res[i], res[j])
-                    add(3, i, j, img[i], img[j])
-                add(1, i, j, dire[i], img[j])
-                add(2, i, j, img[i], res[j])
+                    add_gram(sums, 3, i, j, img[i], img[j])
+                add_gram(sums, 1, i, j, dire[i], img[j])
+                add_gram(sums, 2, i, j, img[i], res[j])
         return carry
 
-    lax.fori_loop(0, lon_blocks, one, 0)
-
-    @pl.when(step == pl.num_programs(0) - 1)
-    def _():
-        lane, row = iota((k, EDGE), 1), iota((k, EDGE), 0)
-        result = jnp.zeros((k, EDGE), F32)
-        for t in range(4):
-            for i in range(k):
-                line = jnp.sum(jnp.sum(sums[t, i], axis=1), axis=1, keepdims=True)
-                line = jnp.broadcast_to(line, (k, EDGE))
-                result = jnp.where(lane == t * k + i, line, result)
-        out_ref[...] = result
+    lax.fori_loop(0, count, one, 0)
+
+
+def gram_total(k, sums):
+    lane = iota((k, EDGE), 1)
+    result = jnp.zeros((k, EDGE), F32)
+    for t in range(4):
+        for i in range(k):
+            line = jnp.sum(jnp.sum(sums[t, i], axis=1), axis=1, keepdims=True)
+            result = jnp.where(lane == t * k + i, jnp.broadcast_to(line, (k, EDGE)), result)
+    return result
 
 
 def flip(x):
@@ -497,24 +546,7 @@
     return b
 
 
-def solve_kernel(bands, part_ref, out_ref, got, send, recv):
-    l = lax.axis_index("lat")
-    greet([{"lat": (l + d) % bands} for d in range(1, bands)])
-
-    def to(d):
-        return pltpu.make_async_remote_copy(
-            src_ref=part_ref, dst_ref=got.at[l], send_sem=send.at[d], recv_sem=recv.at[d],
-            device_id={"lat": (l + d) % bands}, device_id_type=MESH,
-        )
-
-    for d in range(1, bands):
-        to(d).start()
-    got[l] = part_ref[...]
-    for d in range(1, bands):
-        to(d).wait_recv()
-    total = got[0]
-    for d in range(1, bands):
-        total = total + got[d]
+def coefficients(total):
     lane, row = iota((8, EDGE), 1), iota((8, EDGE), 0)
     parts = []
     for t in range(4):
@@ -532,9 +564,7 @@
     cross = product(residual_image, step)
     gram_new = gram_old - cross - flip(cross) + product(flip(step), product(image_image, step))
     turn = solve(gram_old, gram_new)
-    out_ref[...] = jnp.where(lane < 8, step, 0.0) + pltpu.roll(jnp.where(lane < 8, turn, 0.0), 8, 1)
-    for d in range(1, bands):
-        to(d).wait_send()
+    return jnp.where(lane < 8, step, 0.0) + pltpu.roll(jnp.where(lane < 8, turn, 0.0), 8, 1)
 
 
 def update_kernel(k, coef_ref, solution_ref, residual_ref, direction_ref, change_ref, sol_out, res_out, dir_out):
@@ -545,7 +575,7 @@
         for r in range(BAND // rows_each):
             rows = slice(r * rows_each, (r + 1) * rows_each)
             dire = [direction_ref[i, 0, rows, lanes] for i in range(k)]
-            more = [change_block(change_ref, i, b, r * rows_each, rows_each) for i in range(k)]
+            more = [change_block(change_ref, i, 0, b, r * rows_each, rows_each) for i in range(k)]
             for a in range(k):
                 forth = sum(coef_ref[i, a] * dire[i] for i in range(k))
                 back = sum(coef_ref[i, a] * more[i] for i in range(k))
@@ -568,7 +598,7 @@
     k, weeks, band_rows, nlon = direction.shape
     blocks = footprints.shape[2]
     count = nlon // EDGE
-    assert (k, weeks, band_rows, count) == (8, 4, BAND, 5)
+    assert (k, weeks, band_rows, count, bands) == (8, 4, BAND, 5, CHIPS * CHIPS)
     row_blocks = obs_weight.shape[0] // EDGE
     sizes = (bands, weeks, count, (nlon // 8 + 1).bit_length(), band_rows / 2.0, nlon / 32.0)
     l = lax.axis_index("lat")
@@ -588,7 +618,7 @@
             VMEM((weeks, band_rows, nlon), F32), VMEM(plain, F32), VMEM(coded, ints), VMEM((2, *coded), ints), VMEM(plain, BF16),
             DMA((7, weeks)), DMA((7, weeks)), DMA((2, weeks)), DMA((2, weeks)), DMA((weeks,)), DMA((weeks,)),
         ],
-        compiler_params=params(1, 65_000_000),
+        compiler_params=params(1, 64_450_000),
         name="spread",
     )(direction, widths)
 
@@ -631,44 +661,27 @@
         name="adjoint",
     )(block_rows, block_cols, block_scale, values, footprints)
 
-    change = pl.pallas_call(
+    side = CHIPS
+    change, coef = pl.pallas_call(
         functools.partial(image_kernel, sizes),
-        out_shape=jax.ShapeDtypeStruct((k, *coded), ints),
-        in_specs=[ANY_SPEC, VMEM_SPEC],
-        out_specs=ANY_SPEC,
+        out_shape=[jax.ShapeDtypeStruct((k, *coded), ints), jax.ShapeDtypeStruct((k, EDGE), F32)],
+        in_specs=[ANY_SPEC, VMEM_SPEC, ANY_SPEC, ANY_SPEC],
+        out_specs=[ANY_SPEC, VMEM_SPEC],
         scratch_shapes=[
             VMEM((weeks, CHIPS, WEEK, EDGE), F32), VMEM((weeks, CHIPS, WEEK, EDGE), F32),
             *[VMEM(coded, ints)] * 6, VMEM(plain, F32), VMEM(coded, ints), VMEM((2, *coded), ints), VMEM(coded, ints),
+            VMEM((k, *coded), ints), VMEM(direction.shape, F32), VMEM(direction.shape, F32), VMEM((4, k, k, 8, EDGE), F32),
+            VMEM((2, side, k, EDGE), F32), VMEM((2, k, EDGE), F32),
             DMA((7, weeks)), DMA((7, weeks)), DMA((2, weeks)), DMA((2, weeks)), DMA((weeks,)), DMA((weeks,)),
-            DMA((3, weeks)), DMA((3, weeks)), DMA((weeks,)), DMA((weeks,)),
+            DMA((3, weeks)), DMA((3, weeks)), DMA((2, side - 1)), DMA((2, side - 1)), DMA((weeks,)), DMA((weeks,)),
+            DMA((2,)), DMA((weeks,)),
         ],
         compiler_params=params(3),
         name="image",
-    )(part.reshape(CHIPS, 2, *plain), widths)
+    )(part.reshape(CHIPS, 2, *plain), widths, residual, direction)
 
     native = pl.BlockSpec((k, 1, band_rows, nlon), lambda w: (0, w, 0, 0))
     packed = pl.BlockSpec((k, 1, CODED, EDGE), lambda w: (0, w, 0, 0))
-    gram = pl.pallas_call(
-        functools.partial(gram_kernel, k),
-        grid=(weeks,),
-        out_shape=jax.ShapeDtypeStruct((k, EDGE), F32),
-        in_specs=[native, native, packed],
-        out_specs=pl.BlockSpec((k, EDGE), lambda w: (0, 0)),
-        scratch_shapes=[VMEM((4, k, k, 8, EDGE), F32)],
-        compiler_params=params(),
-        name="gram",
-    )(residual, direction, change)
-
-    coef = pl.pallas_call(
-        functools.partial(solve_kernel, bands),
-        out_shape=jax.ShapeDtypeStruct((k, EDGE), F32),
-        in_specs=[VMEM_SPEC],
-        out_specs=VMEM_SPEC,
-        scratch_shapes=[VMEM((bands, k, EDGE), F32), DMA((bands,)), DMA((bands,))],
-        compiler_params=params(4),
-        name="solve",
-    )(gram)
-
     return pl.pallas_call(
         functools.partial(update_kernel, k),
         grid=(weeks,),

time: 127 us -> 119 us (0.937)
  Pallas kernels: 122 us -> 114 us
    pallas_call x3 -> x1, Pallas kernels: 51.6 us -> 43.6 us  [shards(): pl.pallas_call(functools.partial(image_kernel, sizes), out_shape=[jax.Sha...]
where the time goes in v3:
time: 119 us
  Pallas kernels  114 us (96%)
  local copies, waits for them, and re-layouts  2.87 us (2%)
    pallas_call x1, Pallas kernels, shards(): pl.pallas_call(functools.partial(image_kernel, sizes), out_shape=[jax.Sha...  43.6 us
    pallas_call x1, Pallas kernels, shards(): pl.pallas_call(functools.partial(spread_kernel, sizes), out_shape=jax.Sha...  28.8 us
    pallas_call x1, Pallas kernels, shards(): pl.pallas_call(functools.partial(sum_bands_kernel, bands), out_shape=jax....  13.3 us
    pallas_call x1, Pallas kernels, shards(): pl.pallas_call(functools.partial(forward_kernel, per_step), grid=(blocks...  10.1 us
    pallas_call x1, Pallas kernels, shards(): pl.pallas_call(functools.partial(adjoint_kernel, per_step), grid=(blocks...  9.54 us
    pallas_call x1, Pallas kernels, shards(): pl.pallas_call(functools.partial(update_kernel, k), grid=(weeks,), out_sh...  8.88 us

profile of v3, /device:TPU:0, one launch (start us, length us, event | category | flops | bytes accessed | tf_op | source)
XLA Modules:
  0.0 118.5 jit_solution(12874477404110722302)
XLA Ops:
  0.6 0.0 copy-start.6
  0.6 0.0 copy-start.5
  0.7 0.0 copy-start.4
  0.7 0.8 dynamic_slice.6
  1.4 0.8 pad_dynamic-slice_fusion
  2.2 0.6 pad_convert_fusion.widths_ref
  2.8 28.8 %spread.1 = bf16[8,4,160,128]{3,2,1,0:T(8,128)(2,1)} custom-call(f32[8,4,32,640]{3,2,1,0:T(8,128)} %direction_ref.5, f32[8,128]{1,0:T(8,128)} %pad_convert_fusion.widths_ref), custom_call_target="tpu_custom_call" | custom-call | tf_op jit(solution)/shard_map/spread/pallas_call | solution.py:612
  31.6 0.0 copy-done.6
  31.6 0.0 copy-done.5
  31.6 0.0 copy-done.4
  31.6 0.0 copy-start
  31.6 1.3 %copy-done = bf16[8,4,160,128]{3,2,1,0:T(8,128)(2,1)S(1)} copy-done((bf16[8,4,160,128]{3,2,1,0:T(8,128)(2,1)S(1)}, bf16[8,4,160,128]{3,2,1,0:T(8,128)(2,1)}, u32[]{:S(2)}) %copy-start) | copy-done | bytes 1310744
  32.9 0.0 copy-start.3
  32.9 10.1 %forward.1.part_ref = f32[32,8,128]{2,1,0:T(8,128)S(1)} custom-call(s32[1,1,384]{2,1,0:T(1,128)S(1)} %copy-done.4, s32[1,1,384]{2,1,0:T(1,128)S(1)} %copy-done.5, s32[1,1,384]{2,1,0:T(1,128)S(1)} %copy-done.6, bf16[5120,128]{1,0:T(8,128)(2,1)S(1)} %bitcast.8, bf16[1,1,384,128,128]{4,3,2,1,0:T(8,128)(2,1)} %blocks_ref.3), custom_call_target="tpu_custom_call" | custom-call | tf_op jit(solution)/shard_map/forward/pallas_call | solution.py:628
  43.1 0.0 copy-done.3
  43.1 13.3 %sum_bands.1.values_ref = bf16[32,8,128]{2,1,0:T(8,128)(2,1)S(1)} custom-call(f32[32,8,128]{2,1,0:T(8,128)S(1)} %forward.1.part_ref, f32[32,1,128]{2,1,0:T(1,128)S(1)} %bitcast.9), custom_call_target="tpu_custom_call" | custom-call | tf_op jit(solution)/shard_map/sum_bands/pallas_call | solution.py:640
  56.4 0.0 copy-start.2
  56.4 9.5 %adjoint.1 = f32[5120,128]{1,0:T(8,128)S(1)} custom-call(s32[1,1,384]{2,1,0:T(1,128)S(1)} %copy-done.4, s32[1,1,384]{2,1,0:T(1,128)S(1)} %copy-done.5, s32[1,1,384]{2,1,0:T(1,128)S(1)} %copy-done.6, bf16[32,8,128]{2,1,0:T(8,128)(2,1)S(1)} %sum_bands.1.values_ref, bf16[1,1,384,128,128]{4,3,2,1,0:T(8,128)(2,1)} %blocks_ref.3), custom_call_target="tpu_custom_call" | custom-call | tf_op jit(solution)/shard_map/adjoint/pallas_call | solution.py:653
  66.0 0.0 copy-done.2
  66.0 0.0 copy-start.1
  66.0 43.6 %image.1 = (s16[8,4,176,128]{3,2,1,0:T(8,128)(2,1)S(1)}, f32[8,128]{1,0:T(8,128)S(1)}) custom-call(f32[4,2,4,160,128]{4,3,2,1,0:T(8,128)S(1)} %bitcast.7, f32[8,128]{1,0:T(8,128)S(1)} %copy-done.2, f32[8,4,32,640]{3,2,1,0:T(8,128)} %residual_ref.3, f32[8,4,32,640]{3,2,1,0:T(8,128)} %direction_ref.5), custom_call_target="tpu_custom_call" | custom-call | tf_op jit(solution)/shard_map/image/pallas_call | solution.py:665
  109.6 0.0 copy-done.1
  109.7 8.9 %update.1 = (f32[8,4,32,640]{3,2,1,0:T(8,128)}, f32[8,4,32,640]{3,2,1,0:T(8,128)}, f32[8,4,32,640]{3,2,1,0:T(8,128)}) custom-call(f32[8,128]{1,0:T(8,128)S(1)} %get-tuple-element.5.coef_ref, f32[8,4,32,640]{3,2,1,0:T(8,128)S(1)} %copy-done.1, f32[8,4,32,640]{3,2,1,0:T(8,128)} %residual_ref.3, f32[8,4,32,640]{3,2,1,0:T(8,128)} %direction_ref.5, ...), custom_call_target="tpu_custom_call" | custom-call | tf_op jit(solution)/shard_map/update/pallas_call | solution.py:685
  (2 shorter events, 0.0 us)
Async XLA Ops:
  0.6 30.9 %copy-start.6 = (s32[1,1,384]{2,1,0:T(1,128)S(1)}, s32[1,1,384]{2,1,0:T(1,128)}, u32[]{:S(2)}) copy-start(s32[1,1,384]{2,1,0:T(1,128)} %scale_ref.3) | copy-start | bytes 4612
  0.6 30.9 %copy-start.5 = (s32[1,1,384]{2,1,0:T(1,128)S(1)}, s32[1,1,384]{2,1,0:T(1,128)}, u32[]{:S(2)}) copy-start(s32[1,1,384]{2,1,0:T(1,128)} %cols_ref.3) | copy-start | bytes 4612
  0.7 30.9 %copy-start.4 = (s32[1,1,384]{2,1,0:T(1,128)S(1)}, s32[1,1,384]{2,1,0:T(1,128)}, u32[]{:S(2)}) copy-start(s32[1,1,384]{2,1,0:T(1,128)} %rows_ref.3) | copy-start | bytes 4612
  31.6 1.3 %copy-start = (bf16[8,4,160,128]{3,2,1,0:T(8,128)(2,1)S(1)}, bf16[8,4,160,128]{3,2,1,0:T(8,128)(2,1)}, u32[]{:S(2)}) copy-start(bf16[8,4,160,128]{3,2,1,0:T(8,128)(2,1)} %spread.1) | copy-start | bytes 3932164
  32.9 10.2 %copy-start.3 = (f32[4096]{0:T(1024)S(1)}, f32[4096]{0:T(1024)}, u32[]{:S(2)}) copy-start(f32[4096]{0:T(1024)} %param.16) | copy-start | bytes 49156
  56.4 9.6 %copy-start.2 = (f32[8,128]{1,0:T(8,128)S(1)}, f32[8,128]{1,0:T(8,128)}, u32[]{:S(2)}) copy-start(f32[8,128]{1,0:T(8,128)} %pad_convert_fusion.widths_ref) | copy-start | bytes 12292
  66.0 43.7 %copy-start.1 = (f32[8,4,32,640]{3,2,1,0:T(8,128)S(1)}, f32[8,4,32,640]{3,2,1,0:T(8,128)}, u32[]{:S(2)}) copy-start(f32[8,4,32,640]{3,2,1,0:T(8,128)} %solution_ref.1) | copy-start | bytes 7864324

commit v4 on v3

--- a/solution.py
+++ b/solution.py
@@ -35,8 +35,20 @@
     return jnp.sqrt(1.0 + 2.0 * p * (1.0 - jnp.exp(width * (-2.0 / decay))) / (1.0 - p))
 
 
-def down_rows(row):
-    return jnp.transpose(jnp.broadcast_to(row, (EDGE, EDGE)))
+def down_rows(ref, first):
+    row = iota((BAND, EDGE), 0)
+    result = jnp.zeros((BAND, EDGE), jnp.int32)
+    for r in range(BAND):
+        result = jnp.where(row == r, ref[first + r], result)
+    return result.astype(F32)
+
+
+def along_lanes(ref, first, count):
+    lane = iota((1, EDGE), 1)
+    result = jnp.zeros((1, EDGE), jnp.int32)
+    for c in range(count):
+        result = jnp.where(lane == c, ref[(first + c) % ref.shape[0]], result)
+    return result.astype(F32)
 
 
 def along_lon(blocks, width, decay, bits):
@@ -70,7 +82,7 @@
 
 def lat_rows(widths, reach, l, bands, across):
     r, c = iota((BAND, EDGE), 0), iota((BAND, EDGE), 1)
-    width = widths[1:2, :] if across else down_rows(widths[1:2, :])[BAND:2 * BAND]
+    width = along_lanes(widths, (l + bands - 1) * BAND, 3 * BAND) if across else down_rows(widths, l * BAND)
     distance = jnp.abs(r - c + BAND).astype(F32)
     low = jnp.where(l > 0, 0, BAND)
     high = jnp.where(l < bands - 1, 3 * BAND, 2 * BAND)
@@ -187,24 +199,25 @@
 
 
 def run_gather(gather, order, produce, consume):
-    for n, w in enumerate(order):
+    def finish_week(w):
+        gather.complete(w)
+        consume(w)
+
+    a, b, c, d = order
+    for w, late in ((a, None), (b, None), (c, a), (d, b)):
         produce(w)
         gather.send(w)
-        if n >= 1:
-            gather.forward(order[n - 1])
-        if n >= 2:
-            gather.relay(order[n - 2])
-        if n >= 3:
-            gather.complete(order[n - 3])
-            consume(order[n - 3])
-    gather.forward(order[-1])
-    gather.relay(order[-2])
-    gather.complete(order[-3])
-    consume(order[-3])
-    gather.relay(order[-1])
-    for w in order[-2:]:
-        gather.complete(w)
-        consume(w)
+        if late is not None:
+            gather.forward(late)
+    gather.forward(c)
+    gather.relay(a)
+    gather.forward(d)
+    gather.relay(b)
+    finish_week(a)
+    gather.relay(c)
+    gather.relay(d)
+    for w in (b, c, d):
+        finish_week(w)
     gather.finish()
 
 
@@ -228,7 +241,7 @@
         ref[b * BAND:(b + 1) * BAND, :] = value.astype(ref.dtype)
 
 
-def spread_kernel(sizes, direction_ref, widths_ref, out_ref, field, smooth, wire, halo, shard, send, recv, hsend, hrecv, load, local):
+def spread_kernel(sizes, direction_ref, lat_ref, lon_ref, out_ref, field, smooth, wire, halo, shard, send, recv, hsend, hrecv, load, local):
     o, l = lax.axis_index("obs"), lax.axis_index("lat")
     bands, weeks, count, bits, lat_decay, lon_decay = sizes
     loads = [pltpu.make_async_copy(direction_ref.at[o, w], field.at[w], load.at[w]) for w in range(weeks)]
@@ -237,8 +250,8 @@
     z, c, at = obs_peers(o)
     greet([{"obs": at(0, 1 - c)}, {"obs": at(1, c)}, {"obs": at(-1, c)},
            {"lat": (l + 1) % bands}, {"lat": (l + bands - 1) % bands}])
-    lon_width = down_rows(widths_ref[0:1, :])[0:BAND]
-    weights = lat_rows(widths_ref, lat_decay, l, bands, False)
+    lon_width = down_rows(lon_ref, l * BAND)
+    weights = lat_rows(lat_ref, lat_decay, l, bands, False)
     halos = []
 
     def begin(w):
@@ -366,7 +379,7 @@
         second(d, l).wait_send()
 
 
-def image_kernel(sizes, part_ref, widths_ref, residual_ref, direction_ref, out_ref, coef_ref, own, there, far_out, near_out,
+def image_kernel(sizes, part_ref, lat_ref, lon_ref, residual_ref, direction_ref, out_ref, coef_ref, own, there, far_out, near_out,
                  relay_out, far_in, near_in, relay_in, mine, band, halo, shard, everyone, res, dire, sums, line_got, line_sum,
                  send, recv, hsend, hrecv, psend, precv, rsend, rrecv, lsend, lrecv, load, local, fields, leave):
     o, l = lax.axis_index("obs"), lax.axis_index("lat")
@@ -391,8 +404,8 @@
     for one in gets:
         one.start()
     sums[...] = jnp.zeros_like(sums)
-    lon_width = down_rows(widths_ref[0:1, :])[0:BAND]
-    weights = lat_rows(widths_ref, lat_decay, l, bands, True)
+    lon_width = down_rows(lon_ref, l * BAND)
+    weights = lat_rows(lat_ref, lat_decay, l, bands, True)
     ring = (rsend, rrecv)
 
     def way(w):
@@ -601,10 +614,6 @@
     assert (k, weeks, band_rows, count, bands) == (8, 4, BAND, 5, CHIPS * CHIPS)
     row_blocks = obs_weight.shape[0] // EDGE
     sizes = (bands, weeks, count, (nlon // 8 + 1).bit_length(), band_rows / 2.0, nlon / 32.0)
-    l = lax.axis_index("lat")
-    lon_own = lax.dynamic_slice_in_dim(lon_width, l * BAND, BAND)
-    lat_near = lax.dynamic_slice_in_dim(jnp.pad(lat_width, BAND), l * BAND, 3 * BAND)
-    widths = jnp.pad(jnp.stack([jnp.pad(lon_own, (0, 3 * BAND)), jnp.pad(lat_near, (0, BAND))]), ((0, 6), (0, 0))).astype(F32)
     all_rows = k * weeks * WEEK
     plain, coded = (weeks, WEEK, EDGE), (weeks, CODED, EDGE)
     ints = jnp.int16
@@ -612,7 +621,7 @@
     cells = pl.pallas_call(
         functools.partial(spread_kernel, sizes),
         out_shape=jax.ShapeDtypeStruct((k, *plain), BF16),
-        in_specs=[ANY_SPEC, VMEM_SPEC],
+        in_specs=[ANY_SPEC, SMEM_SPEC, SMEM_SPEC],
         out_specs=ANY_SPEC,
         scratch_shapes=[
             VMEM((weeks, band_rows, nlon), F32), VMEM(plain, F32), VMEM(coded, ints), VMEM((2, *coded), ints), VMEM(plain, BF16),
@@ -620,9 +629,9 @@
         ],
         compiler_params=params(1, 64_450_000),
         name="spread",
-    )(direction, widths)
-
-    per_step = 48
+    )(direction, lat_width, lon_width)
+
+    per_step = 64
     smem = [SMEM_SPEC] * 3
     block_spec = pl.BlockSpec((None, None, per_step, EDGE, EDGE), lambda i: (0, 0, i, 0, 0))
     forward = pl.pallas_call(
@@ -632,7 +641,7 @@
         in_specs=smem + [pl.BlockSpec((all_rows, EDGE), lambda i: (0, 0)), block_spec],
         out_specs=pl.BlockSpec((row_blocks, k, EDGE), lambda i: (0, 0, 0)),
         scratch_shapes=[VMEM((k * STEP, EDGE), F32)],
-        compiler_params=params(),
+        compiler_params=params(None, 66_000_000),
         name="forward",
     )(block_rows, block_cols, block_scale, cells.reshape(all_rows, EDGE), footprints)
 
@@ -665,7 +674,7 @@
     change, coef = pl.pallas_call(
         functools.partial(image_kernel, sizes),
         out_shape=[jax.ShapeDtypeStruct((k, *coded), ints), jax.ShapeDtypeStruct((k, EDGE), F32)],
-        in_specs=[ANY_SPEC, VMEM_SPEC, ANY_SPEC, ANY_SPEC],
+        in_specs=[ANY_SPEC, SMEM_SPEC, SMEM_SPEC, ANY_SPEC, ANY_SPEC],
         out_specs=[ANY_SPEC, VMEM_SPEC],
         scratch_shapes=[
             VMEM((weeks, CHIPS, WEEK, EDGE), F32), VMEM((weeks, CHIPS, WEEK, EDGE), F32),
@@ -678,7 +687,7 @@
         ],
         compiler_params=params(3),
         name="image",
-    )(part.reshape(CHIPS, 2, *plain), widths, residual, direction)
+    )(part.reshape(CHIPS, 2, *plain), lat_width, lon_width, residual, direction)
 
     native = pl.BlockSpec((k, 1, band_rows, nlon), lambda w: (0, w, 0, 0))
     packed = pl.BlockSpec((k, 1, CODED, EDGE), lambda w: (0, w, 0, 0))

time: 119 us -> 113 us (0.950)
  Pallas kernels: 114 us -> 111 us
  local copies, waits for them, and re-layouts: 2.87 us -> 0.95 us
    pallas_call x1, Pallas kernels: 43.6 us -> 41.2 us  [shards(): pl.pallas_call(functools.partial(image_kernel, sizes), out_shape=[jax.Sha...]
    dynamic_slice x2 -> x0, local copies, waits for them, and re-layouts: 1.52 us -> none  [the longest x1 0.77 us: shards(): lon_own = lax.dynamic_slice_in_dim(lon_width, l * BAND, BAND)]
where the time goes in v4:
time: 113 us; the launch traced here: 112 us
  Pallas kernels  111 us (98%)
    pallas_call x1, Pallas kernels, shards(): pl.pallas_call(functools.partial(image_kernel, sizes), out_shape=[jax.Sha...  41.2 us
    pallas_call x1, Pallas kernels, shards(): pl.pallas_call(functools.partial(spread_kernel, sizes), out_shape=jax.Sha...  28.5 us
    pallas_call x1, Pallas kernels, shards(): pl.pallas_call(functools.partial(sum_bands_kernel, bands), out_shape=jax....  12.5 us
    pallas_call x1, Pallas kernels, shards(): pl.pallas_call(functools.partial(forward_kernel, per_step), grid=(blocks...  10.6 us
    pallas_call x1, Pallas kernels, shards(): pl.pallas_call(functools.partial(update_kernel, k), grid=(weeks,), out_sh...  8.88 us
    pallas_call x1, Pallas kernels, shards(): pl.pallas_call(functools.partial(adjoint_kernel, per_step), grid=(blocks...  8.8 us

profile of v4, /device:TPU:0, one launch (start us, length us, event | category | flops | bytes accessed | tf_op | source)
XLA Modules:
  0.0 112.3 jit_solution(17867432093473637962)
XLA Ops:
  0.6 28.5 %spread.1 = bf16[8,4,160,128]{3,2,1,0:T(8,128)(2,1)} custom-call(f32[8,4,32,640]{3,2,1,0:T(8,128)} %direction_ref.5, s32[512]{0:T(512)} %lat_ref.3, s32[512]{0:T(512)} %lon_ref.3), custom_call_target="tpu_custom_call" | custom-call | tf_op jit(solution)/shard_map/spread/pallas_call | solution.py:621
  29.1 0.0 copy-start.2
  29.1 0.0 copy-start.5
  29.1 0.0 copy-start.6
  29.1 0.0 copy-start.7
  29.1 10.6 %forward.1.part_ref = f32[32,8,128]{2,1,0:T(8,128)} custom-call(s32[1,1,384]{2,1,0:T(1,128)} %rows_ref.3, s32[1,1,384]{2,1,0:T(1,128)} %cols_ref.3, s32[1,1,384]{2,1,0:T(1,128)} %scale_ref.3, bf16[5120,128]{1,0:T(8,128)(2,1)} %bitcast.5, bf16[1,1,384,128,128]{4,3,2,1,0:T(8,128)(2,1)} %blocks_ref.3), custom_call_target="tpu_custom_call" | custom-call | tf_op jit(solution)/shard_map/forward/pallas_call | solution.py:637
  39.8 0.0 copy-done.2
  39.8 0.0 copy-start.1
  39.8 0.9 copy-done.1
  40.7 12.5 %sum_bands.1.values_ref = bf16[32,8,128]{2,1,0:T(8,128)(2,1)S(1)} custom-call(f32[32,8,128]{2,1,0:T(8,128)S(1)} %copy-done.1, f32[32,1,128]{2,1,0:T(1,128)S(1)} %bitcast.4), custom_call_target="tpu_custom_call" | custom-call | tf_op jit(solution)/shard_map/sum_bands/pallas_call | solution.py:649
  53.2 0.0 copy-done.5
  53.2 0.0 copy-done.6
  53.2 0.0 copy-done.7
  53.2 0.0 copy-start.3
  53.3 0.0 copy-start.4
  53.3 8.8 %adjoint.1 = f32[5120,128]{1,0:T(8,128)S(1)} custom-call(s32[1,1,384]{2,1,0:T(1,128)S(1)} %copy-done.5, s32[1,1,384]{2,1,0:T(1,128)S(1)} %copy-done.6, s32[1,1,384]{2,1,0:T(1,128)S(1)} %copy-done.7, bf16[32,8,128]{2,1,0:T(8,128)(2,1)S(1)} %sum_bands.1.values_ref, bf16[1,1,384,128,128]{4,3,2,1,0:T(8,128)(2,1)} %blocks_ref.3), custom_call_target="tpu_custom_call" | custom-call | tf_op jit(solution)/shard_map/adjoint/pallas_call | solution.py:662
  62.1 0.0 copy-done.3
  62.1 0.0 copy-done.4
  62.1 0.0 copy-start
  62.1 41.2 %image.1 = (s16[8,4,176,128]{3,2,1,0:T(8,128)(2,1)S(1)}, f32[8,128]{1,0:T(8,128)S(1)}) custom-call(f32[4,2,4,160,128]{4,3,2,1,0:T(8,128)S(1)} %bitcast.3, s32[512]{0:T(512)S(1)} %copy-done.3, s32[512]{0:T(512)S(1)} %copy-done.4, f32[8,4,32,640]{3,2,1,0:T(8,128)} %residual_ref.3, f32[8,4,32,640]{3,2,1,0:T(8,128)} %direction_ref.5), custom_call_target="tpu_custom_call" | custom-call | tf_op jit(solution)/shard_map/image/pallas_call | solution.py:674
  103.4 0.0 copy-done
  103.4 8.9 %update.1 = (f32[8,4,32,640]{3,2,1,0:T(8,128)}, f32[8,4,32,640]{3,2,1,0:T(8,128)}, f32[8,4,32,640]{3,2,1,0:T(8,128)}) custom-call(f32[8,128]{1,0:T(8,128)S(1)} %get-tuple-element.5.coef_ref, f32[8,4,32,640]{3,2,1,0:T(8,128)S(1)} %copy-done, f32[8,4,32,640]{3,2,1,0:T(8,128)} %residual_ref.3, f32[8,4,32,640]{3,2,1,0:T(8,128)} %direction_ref.5, ...), custom_call_target="tpu_custom_call" | custom-call | tf_op jit(solution)/shard_map/update/pallas_call | solution.py:694
Async XLA Ops:
  29.1 10.7 %copy-start.2 = (f32[4096]{0:T(1024)S(1)}, f32[4096]{0:T(1024)}, u32[]{:S(2)}) copy-start(f32[4096]{0:T(1024)} %param.16) | copy-start | bytes 49156
  29.1 24.1 %copy-start.5 = (s32[1,1,384]{2,1,0:T(1,128)S(1)}, s32[1,1,384]{2,1,0:T(1,128)}, u32[]{:S(2)}) copy-start(s32[1,1,384]{2,1,0:T(1,128)} %rows_ref.3) | copy-start | bytes 4612
  29.1 24.1 %copy-start.6 = (s32[1,1,384]{2,1,0:T(1,128)S(1)}, s32[1,1,384]{2,1,0:T(1,128)}, u32[]{:S(2)}) copy-start(s32[1,1,384]{2,1,0:T(1,128)} %cols_ref.3) | copy-start | bytes 4612
  29.1 24.1 %copy-start.7 = (s32[1,1,384]{2,1,0:T(1,128)S(1)}, s32[1,1,384]{2,1,0:T(1,128)}, u32[]{:S(2)}) copy-start(s32[1,1,384]{2,1,0:T(1,128)} %scale_ref.3) | copy-start | bytes 4612
  39.8 0.9 copy-start.1
  53.2 8.8 %copy-start.3 = (s32[512]{0:T(512)S(1)}, s32[512]{0:T(512)}, u32[]{:S(2)}) copy-start(s32[512]{0:T(512)} %lat_ref.3) | copy-start | bytes 6148
  53.3 8.8 %copy-start.4 = (s32[512]{0:T(512)S(1)}, s32[512]{0:T(512)}, u32[]{:S(2)}) copy-start(s32[512]{0:T(512)} %lon_ref.3) | copy-start | bytes 6148
  62.1 41.3 %copy-start = (f32[8,4,32,640]{3,2,1,0:T(8,128)S(1)}, f32[8,4,32,640]{3,2,1,0:T(8,128)}, u32[]{:S(2)}) copy-start(f32[8,4,32,640]{3,2,1,0:T(8,128)} %solution_ref.1) | copy-start | bytes 7864324

commit v5 on v4

--- a/solution.py
+++ b/solution.py
@@ -294,39 +294,54 @@
     return (8 >> scale).astype(F32) * 0.125
 
 
-def forward_kernel(per_step, rows_ref, cols_ref, scale_ref, cells_ref, blocks_ref, out_ref, cells):
-    step = pl.program_id(0)
-
-    @pl.when(step == 0)
-    def _():
+CHUNK = 32
+
+
+def all_pairs(blocks_ref, held, sems, two, before=None):
+    chunks = held.shape[0] // CHUNK
+
+    def fetch(i):
+        some = pl.ds(i * CHUNK, CHUNK)
+        return pltpu.make_async_copy(blocks_ref.at[0, 0, some], held.at[some], sems.at[i])
+
+    for i in range(chunks):
+        fetch(i).start()
+    before()
+
+    def chunk(i, carry):
+        fetch(i).wait()
+        return lax.fori_loop(0, CHUNK // 2, lambda n, c: two(i * (CHUNK // 2) + n, c), carry, unroll=8)
+
+    lax.fori_loop(0, chunks, chunk, 0)
+
+
+def forward_kernel(rows_ref, cols_ref, scale_ref, cells_ref, blocks_ref, out_ref, cells, held, sems):
+    def before():
         for k in range(8):
             cells[k * STEP:k * STEP + FIELD, :] = cells_ref[k * FIELD:(k + 1) * FIELD, :].astype(F32)
         out_ref[...] = jnp.zeros_like(out_ref)
 
     def two(n, carry):
-        at = [step * per_step + 2 * n + i for i in range(2)]
+        at = [2 * n + i for i in range(2)]
         picked = pair(*[cells[place_of(cols_ref[0, 0, a]), :].astype(BF16) for a in at])
-        both = jnp.concatenate([blocks_ref[2 * n], blocks_ref[2 * n + 1]], axis=1)
+        both = jnp.concatenate([held[a] for a in at], axis=1)
         value = lax.dot_general(picked, both, (((1,), (1,)), ((), ())), preferred_element_type=F32)
         for i, a in enumerate(at):
             row = rows_ref[0, 0, a]
             out_ref[row] = out_ref[row] + value[8 * i:8 * i + 8] * factor_of(scale_ref[0, 0, a])
         return carry
 
-    lax.fori_loop(0, per_step // 2, two, 0, unroll=8)
-
-
-def adjoint_kernel(per_step, rows_ref, cols_ref, scale_ref, values_ref, blocks_ref, out_ref, total):
-    step = pl.program_id(0)
-
-    @pl.when(step == 0)
-    def _():
+    all_pairs(blocks_ref, held, sems, two, before)
+
+
+def adjoint_kernel(rows_ref, cols_ref, scale_ref, values_ref, blocks_ref, out_ref, total, held, sems):
+    def before():
         total[...] = jnp.zeros_like(total)
 
     def two(n, carry):
-        at = [step * per_step + 2 * n + i for i in range(2)]
+        at = [2 * n + i for i in range(2)]
         pulled = jnp.concatenate([values_ref[rows_ref[0, 0, a]] for a in at], axis=0)
-        both = jnp.concatenate([blocks_ref[2 * n], blocks_ref[2 * n + 1]], axis=1)
+        both = jnp.concatenate([held[a] for a in at], axis=1)
         value = jnp.dot(pulled, both, preferred_element_type=F32)
         for i, a in enumerate(at):
             place = place_of(cols_ref[0, 0, a])
@@ -334,12 +349,9 @@
             total[place, :] = total[place, :] + part * factor_of(scale_ref[0, 0, a])
         return carry
 
-    lax.fori_loop(0, per_step // 2, two, 0, unroll=8)
-
-    @pl.when(step == pl.num_programs(0) - 1)
-    def _():
-        for k in range(8):
-            out_ref[k * FIELD:(k + 1) * FIELD, :] = total[k * STEP:k * STEP + FIELD, :]
+    all_pairs(blocks_ref, held, sems, two, before)
+    for k in range(8):
+        out_ref[k * FIELD:(k + 1) * FIELD, :] = total[k * STEP:k * STEP + FIELD, :]
 
 
 def sum_bands_kernel(bands, part_ref, weight_ref, out_ref, got, shard, send, recv, send2, recv2):
@@ -574,9 +586,10 @@
     curvature = 0.5 * (parts[1] + flip(parts[1]))
     residual_image = parts[2]
     step = solve(curvature, gram_old)
+    inverse = solve(gram_old, jnp.where(lane == row, 1.0, 0.0))
     cross = product(residual_image, step)
     gram_new = gram_old - cross - flip(cross) + product(flip(step), product(image_image, step))
-    turn = solve(gram_old, gram_new)
+    turn = product(inverse, gram_new)
     return jnp.where(lane < 8, step, 0.0) + pltpu.roll(jnp.where(lane < 8, turn, 0.0), 8, 1)
 
 
@@ -631,17 +644,15 @@
         name="spread",
     )(direction, lat_width, lon_width)
 
-    per_step = 64
+    blocks_held = [VMEM((blocks, EDGE, EDGE), BF16), DMA((blocks // CHUNK,))]
     smem = [SMEM_SPEC] * 3
-    block_spec = pl.BlockSpec((None, None, per_step, EDGE, EDGE), lambda i: (0, 0, i, 0, 0))
     forward = pl.pallas_call(
-        functools.partial(forward_kernel, per_step),
-        grid=(blocks // per_step,),
+        forward_kernel,
         out_shape=jax.ShapeDtypeStruct((row_blocks, k, EDGE), F32),
-        in_specs=smem + [pl.BlockSpec((all_rows, EDGE), lambda i: (0, 0)), block_spec],
-        out_specs=pl.BlockSpec((row_blocks, k, EDGE), lambda i: (0, 0, 0)),
-        scratch_shapes=[VMEM((k * STEP, EDGE), F32)],
-        compiler_params=params(None, 66_000_000),
+        in_specs=smem + [VMEM_SPEC, ANY_SPEC],
+        out_specs=VMEM_SPEC,
+        scratch_shapes=[VMEM((k * STEP, EDGE), F32), *blocks_held],
+        compiler_params=params(),
         name="forward",
     )(block_rows, block_cols, block_scale, cells.reshape(all_rows, EDGE), footprints)
 
@@ -660,12 +671,11 @@
     )(forward, obs_weight.reshape(row_blocks, 1, EDGE))
 
     part = pl.pallas_call(
-        functools.partial(adjoint_kernel, per_step),
-        grid=(blocks // per_step,),
+        adjoint_kernel,
         out_shape=jax.ShapeDtypeStruct((all_rows, EDGE), F32),
-        in_specs=smem + [pl.BlockSpec((row_blocks, k, EDGE), lambda i: (0, 0, 0)), block_spec],
-        out_specs=pl.BlockSpec((all_rows, EDGE), lambda i: (0, 0)),
-        scratch_shapes=[VMEM((k * STEP, EDGE), F32)],
+        in_specs=smem + [VMEM_SPEC, ANY_SPEC],
+        out_specs=VMEM_SPEC,
+        scratch_shapes=[VMEM((k * STEP, EDGE), F32), *blocks_held],
         compiler_params=params(),
         name="adjoint",
     )(block_rows, block_cols, block_scale, values, footprints)

time: 113 us -> 109 us (0.965)
  Pallas kernels: 111 us -> 107 us
    pallas_call x2, Pallas kernels: 19.4 us -> 15.2 us  [the longest x1 8.21 us: shards(): pl.pallas_call(forward_kernel, out_shape=jax.ShapeDtypeStruct((row_blocks...]
where the time goes in v5:
time: 109 us
  Pallas kernels  107 us (98%)
  local copies, waits for them, and re-layouts  1.34 us (1%)
    pallas_call x1, Pallas kernels, shards(): pl.pallas_call(functools.partial(image_kernel, sizes), out_shape=[jax.Sha...  41.3 us
    pallas_call x1, Pallas kernels, shards(): pl.pallas_call(functools.partial(spread_kernel, sizes), out_shape=jax.Sha...  28.5 us
    pallas_call x1, Pallas kernels, shards(): pl.pallas_call(functools.partial(sum_bands_kernel, bands), out_shape=jax....  12.7 us
    pallas_call x1, Pallas kernels, shards(): pl.pallas_call(functools.partial(update_kernel, k), grid=(weeks,), out_sh...  8.88 us
    pallas_call x1, Pallas kernels, shards(): pl.pallas_call(forward_kernel, out_shape=jax.ShapeDtypeStruct((row_blocks...  8.21 us
    pallas_call x1, Pallas kernels, shards(): pl.pallas_call(adjoint_kernel, out_shape=jax.ShapeDtypeStruct((all_rows,...  7.03 us

profile of v5, /device:TPU:0, one launch (start us, length us, event | category | flops | bytes accessed | tf_op | source)
XLA Modules:
  0.0 108.7 jit_solution(9845113837039429127)
XLA Ops:
  0.6 0.0 copy-start.7
  0.6 0.0 copy-start.6
  0.7 0.0 copy-start.5
  0.7 28.5 %spread.1 = bf16[8,4,160,128]{3,2,1,0:T(8,128)(2,1)} custom-call(f32[8,4,32,640]{3,2,1,0:T(8,128)} %direction_ref.5, s32[512]{0:T(512)} %lat_ref.3, s32[512]{0:T(512)} %lon_ref.3), custom_call_target="tpu_custom_call" | custom-call | tf_op jit(solution)/shard_map/spread/pallas_call | solution.py:634
  29.1 0.0 copy-done.7
  29.1 0.0 copy-done.6
  29.1 0.0 copy-done.5
  29.2 0.0 copy-start
  29.2 1.3 %copy-done = bf16[8,4,160,128]{3,2,1,0:T(8,128)(2,1)S(1)} copy-done((bf16[8,4,160,128]{3,2,1,0:T(8,128)(2,1)S(1)}, bf16[8,4,160,128]{3,2,1,0:T(8,128)(2,1)}, u32[]{:S(2)}) %copy-start) | copy-done | bytes 1310744
  30.5 0.0 copy-start.2
  30.5 8.2 %forward.1.part_ref = f32[32,8,128]{2,1,0:T(8,128)S(1)} custom-call(s32[1,1,384]{2,1,0:T(1,128)S(1)} %copy-done.5, s32[1,1,384]{2,1,0:T(1,128)S(1)} %copy-done.6, s32[1,1,384]{2,1,0:T(1,128)S(1)} %copy-done.7, bf16[5120,128]{1,0:T(8,128)(2,1)S(1)} %bitcast.4, bf16[1,1,384,128,128]{4,3,2,1,0:T(8,128)(2,1)} %blocks_ref.3), custom_call_target="tpu_custom_call" | custom-call | tf_op jit(solution)/shard_map/forward/pallas_call | solution.py:649
  38.7 0.0 copy-done.2
  38.7 12.7 %sum_bands.1.values_ref = bf16[32,8,128]{2,1,0:T(8,128)(2,1)S(1)} custom-call(f32[32,8,128]{2,1,0:T(8,128)S(1)} %forward.1.part_ref, f32[32,1,128]{2,1,0:T(1,128)S(1)} %bitcast.5), custom_call_target="tpu_custom_call" | custom-call | tf_op jit(solution)/shard_map/sum_bands/pallas_call | solution.py:660
  51.4 0.0 copy-start.3
  51.4 0.0 copy-start.4
  51.4 7.0 %adjoint.1 = f32[5120,128]{1,0:T(8,128)S(1)} custom-call(s32[1,1,384]{2,1,0:T(1,128)S(1)} %copy-done.5, s32[1,1,384]{2,1,0:T(1,128)S(1)} %copy-done.6, s32[1,1,384]{2,1,0:T(1,128)S(1)} %copy-done.7, bf16[32,8,128]{2,1,0:T(8,128)(2,1)S(1)} %sum_bands.1.values_ref, bf16[1,1,384,128,128]{4,3,2,1,0:T(8,128)(2,1)} %blocks_ref.3), custom_call_target="tpu_custom_call" | custom-call | tf_op jit(solution)/shard_map/adjoint/pallas_call | solution.py:673
  58.5 0.0 copy-done.3
  58.5 0.0 copy-done.4
  58.5 0.0 copy-start.1
  58.5 41.3 %image.1 = (s16[8,4,176,128]{3,2,1,0:T(8,128)(2,1)S(1)}, f32[8,128]{1,0:T(8,128)S(1)}) custom-call(f32[4,2,4,160,128]{4,3,2,1,0:T(8,128)S(1)} %bitcast.3, s32[512]{0:T(512)S(1)} %copy-done.3, s32[512]{0:T(512)S(1)} %copy-done.4, f32[8,4,32,640]{3,2,1,0:T(8,128)} %residual_ref.3, f32[8,4,32,640]{3,2,1,0:T(8,128)} %direction_ref.5), custom_call_target="tpu_custom_call" | custom-call | tf_op jit(solution)/shard_map/image/pallas_call | solution.py:684
  99.8 0.0 copy-done.1
  99.8 8.9 %update.1 = (f32[8,4,32,640]{3,2,1,0:T(8,128)}, f32[8,4,32,640]{3,2,1,0:T(8,128)}, f32[8,4,32,640]{3,2,1,0:T(8,128)}) custom-call(f32[8,128]{1,0:T(8,128)S(1)} %get-tuple-element.5.coef_ref, f32[8,4,32,640]{3,2,1,0:T(8,128)S(1)} %copy-done.1, f32[8,4,32,640]{3,2,1,0:T(8,128)} %residual_ref.3, f32[8,4,32,640]{3,2,1,0:T(8,128)} %direction_ref.5, ...), custom_call_target="tpu_custom_call" | custom-call | tf_op jit(solution)/shard_map/update/pallas_call | solution.py:704
Async XLA Ops:
  0.6 28.5 %copy-start.7 = (s32[1,1,384]{2,1,0:T(1,128)S(1)}, s32[1,1,384]{2,1,0:T(1,128)}, u32[]{:S(2)}) copy-start(s32[1,1,384]{2,1,0:T(1,128)} %scale_ref.3) | copy-start | bytes 4612
  0.6 28.5 %copy-start.6 = (s32[1,1,384]{2,1,0:T(1,128)S(1)}, s32[1,1,384]{2,1,0:T(1,128)}, u32[]{:S(2)}) copy-start(s32[1,1,384]{2,1,0:T(1,128)} %cols_ref.3) | copy-start | bytes 4612
  0.7 28.5 %copy-start.5 = (s32[1,1,384]{2,1,0:T(1,128)S(1)}, s32[1,1,384]{2,1,0:T(1,128)}, u32[]{:S(2)}) copy-start(s32[1,1,384]{2,1,0:T(1,128)} %rows_ref.3) | copy-start | bytes 4612
  29.2 1.3 %copy-start = (bf16[8,4,160,128]{3,2,1,0:T(8,128)(2,1)S(1)}, bf16[8,4,160,128]{3,2,1,0:T(8,128)(2,1)}, u32[]{:S(2)}) copy-start(bf16[8,4,160,128]{3,2,1,0:T(8,128)(2,1)} %spread.1) | copy-start | bytes 3932164
  30.5 8.2 %copy-start.2 = (f32[4096]{0:T(1024)S(1)}, f32[4096]{0:T(1024)}, u32[]{:S(2)}) copy-start(f32[4096]{0:T(1024)} %param.16) | copy-start | bytes 49156
  51.4 7.1 %copy-start.3 = (s32[512]{0:T(512)S(1)}, s32[512]{0:T(512)}, u32[]{:S(2)}) copy-start(s32[512]{0:T(512)} %lat_ref.3) | copy-start | bytes 6148
  51.4 7.1 %copy-start.4 = (s32[512]{0:T(512)S(1)}, s32[512]{0:T(512)}, u32[]{:S(2)}) copy-start(s32[512]{0:T(512)} %lon_ref.3) | copy-start | bytes 6148
  58.5 41.4 %copy-start.1 = (f32[8,4,32,640]{3,2,1,0:T(8,128)S(1)}, f32[8,4,32,640]{3,2,1,0:T(8,128)}, u32[]{:S(2)}) copy-start(f32[8,4,32,640]{3,2,1,0:T(8,128)} %solution_ref.1) | copy-start | bytes 7864324

commit v6 on v5

--- a/solution.py
+++ b/solution.py
@@ -357,7 +357,8 @@
 def sum_bands_kernel(bands, part_ref, weight_ref, out_ref, got, shard, send, recv, send2, recv2):
     l = lax.axis_index("lat")
     share = part_ref.shape[0] // bands
-    greet([{"lat": (l + d) % bands} for d in range(1, bands)])
+    far_first = (10, 6, 9, 11, 14, 2, 8, 5, 7, 13, 3, 15, 12, 1, 4)
+    greet([{"lat": (l + d) % bands} for d in far_first])
     mine = pl.ds(l * share, share)
 
     def first(d):
@@ -373,18 +374,18 @@
             device_id={"lat": (l + d) % bands}, device_id_type=MESH,
         )
 
-    for d in range(1, bands):
+    for d in far_first:
         first(d).start()
     total = part_ref[mine]
-    for d in range(1, bands):
+    for d in far_first[::-1]:
         first(d).wait_recv()
         total = total + got[d]
     weight = weight_ref[mine]
     shard[...] = (total * weight).astype(shard.dtype)
-    for d in range(1, bands):
+    for d in far_first:
         second(d, l).start()
     out_ref[mine] = shard[...]
-    for d in range(1, bands):
+    for d in far_first[::-1]:
         second(d, (l + bands - d) % bands).wait_recv()
     for d in range(1, bands):
         first(d).wait_send()

time: 109 us -> 108 us (level)
  no operation moved by 1% of the time
where the time goes in v6:
time: 108 us
  Pallas kernels  106 us (98%)
  local copies, waits for them, and re-layouts  1.34 us (1%)
    pallas_call x1, Pallas kernels, shards(): pl.pallas_call(functools.partial(image_kernel, sizes), out_shape=[jax.Sha...  41.1 us
    pallas_call x1, Pallas kernels, shards(): pl.pallas_call(functools.partial(spread_kernel, sizes), out_shape=jax.Sha...  28.5 us
    pallas_call x1, Pallas kernels, shards(): pl.pallas_call(functools.partial(sum_bands_kernel, bands), out_shape=jax....  12.4 us
    pallas_call x1, Pallas kernels, shards(): pl.pallas_call(functools.partial(update_kernel, k), grid=(weeks,), out_sh...  8.88 us
    pallas_call x1, Pallas kernels, shards(): pl.pallas_call(forward_kernel, out_shape=jax.ShapeDtypeStruct((row_blocks...  8.2 us
    pallas_call x1, Pallas kernels, shards(): pl.pallas_call(adjoint_kernel, out_shape=jax.ShapeDtypeStruct((all_rows,...  7.03 us

profile of v6, /device:TPU:0, one launch (start us, length us, event | category | flops | bytes accessed | tf_op | source)
XLA Modules:
  0.0 108.2 jit_solution(6434153814551576545)
XLA Ops:
  0.6 0.0 copy-start.7
  0.6 0.0 copy-start.6
  0.7 0.0 copy-start.5
  0.7 28.5 %spread.1 = bf16[8,4,160,128]{3,2,1,0:T(8,128)(2,1)} custom-call(f32[8,4,32,640]{3,2,1,0:T(8,128)} %direction_ref.5, s32[512]{0:T(512)} %lat_ref.3, s32[512]{0:T(512)} %lon_ref.3), custom_call_target="tpu_custom_call" | custom-call | tf_op jit(solution)/shard_map/spread/pallas_call | solution.py:635
  29.1 0.0 copy-done.7
  29.1 0.0 copy-done.6
  29.1 0.0 copy-done.5
  29.2 0.0 copy-start
  29.2 1.3 %copy-done = bf16[8,4,160,128]{3,2,1,0:T(8,128)(2,1)S(1)} copy-done((bf16[8,4,160,128]{3,2,1,0:T(8,128)(2,1)S(1)}, bf16[8,4,160,128]{3,2,1,0:T(8,128)(2,1)}, u32[]{:S(2)}) %copy-start) | copy-done | bytes 1310744
  30.5 0.0 copy-start.2
  30.5 8.2 %forward.1.part_ref = f32[32,8,128]{2,1,0:T(8,128)S(1)} custom-call(s32[1,1,384]{2,1,0:T(1,128)S(1)} %copy-done.5, s32[1,1,384]{2,1,0:T(1,128)S(1)} %copy-done.6, s32[1,1,384]{2,1,0:T(1,128)S(1)} %copy-done.7, bf16[5120,128]{1,0:T(8,128)(2,1)S(1)} %bitcast.4, bf16[1,1,384,128,128]{4,3,2,1,0:T(8,128)(2,1)} %blocks_ref.3), custom_call_target="tpu_custom_call" | custom-call | tf_op jit(solution)/shard_map/forward/pallas_call | solution.py:650
  38.7 0.0 copy-done.2
  38.7 12.4 %sum_bands.1.values_ref = bf16[32,8,128]{2,1,0:T(8,128)(2,1)S(1)} custom-call(f32[32,8,128]{2,1,0:T(8,128)S(1)} %forward.1.part_ref, f32[32,1,128]{2,1,0:T(1,128)S(1)} %bitcast.5), custom_call_target="tpu_custom_call" | custom-call | tf_op jit(solution)/shard_map/sum_bands/pallas_call | solution.py:661
  51.1 0.0 copy-start.3
  51.1 0.0 copy-start.4
  51.2 7.0 %adjoint.1 = f32[5120,128]{1,0:T(8,128)S(1)} custom-call(s32[1,1,384]{2,1,0:T(1,128)S(1)} %copy-done.5, s32[1,1,384]{2,1,0:T(1,128)S(1)} %copy-done.6, s32[1,1,384]{2,1,0:T(1,128)S(1)} %copy-done.7, bf16[32,8,128]{2,1,0:T(8,128)(2,1)S(1)} %sum_bands.1.values_ref, bf16[1,1,384,128,128]{4,3,2,1,0:T(8,128)(2,1)} %blocks_ref.3), custom_call_target="tpu_custom_call" | custom-call | tf_op jit(solution)/shard_map/adjoint/pallas_call | solution.py:674
  58.2 0.0 copy-done.3
  58.2 0.0 copy-done.4
  58.2 0.0 copy-start.1
  58.2 41.1 %image.1 = (s16[8,4,176,128]{3,2,1,0:T(8,128)(2,1)S(1)}, f32[8,128]{1,0:T(8,128)S(1)}) custom-call(f32[4,2,4,160,128]{4,3,2,1,0:T(8,128)S(1)} %bitcast.3, s32[512]{0:T(512)S(1)} %copy-done.3, s32[512]{0:T(512)S(1)} %copy-done.4, f32[8,4,32,640]{3,2,1,0:T(8,128)} %residual_ref.3, f32[8,4,32,640]{3,2,1,0:T(8,128)} %direction_ref.5), custom_call_target="tpu_custom_call" | custom-call | tf_op jit(solution)/shard_map/image/pallas_call | solution.py:685
  99.3 0.0 copy-done.1
  99.3 8.9 %update.1 = (f32[8,4,32,640]{3,2,1,0:T(8,128)}, f32[8,4,32,640]{3,2,1,0:T(8,128)}, f32[8,4,32,640]{3,2,1,0:T(8,128)}) custom-call(f32[8,128]{1,0:T(8,128)S(1)} %get-tuple-element.5.coef_ref, f32[8,4,32,640]{3,2,1,0:T(8,128)S(1)} %copy-done.1, f32[8,4,32,640]{3,2,1,0:T(8,128)} %residual_ref.3, f32[8,4,32,640]{3,2,1,0:T(8,128)} %direction_ref.5, ...), custom_call_target="tpu_custom_call" | custom-call | tf_op jit(solution)/shard_map/update/pallas_call | solution.py:705
Async XLA Ops:
  0.6 28.5 %copy-start.7 = (s32[1,1,384]{2,1,0:T(1,128)S(1)}, s32[1,1,384]{2,1,0:T(1,128)}, u32[]{:S(2)}) copy-start(s32[1,1,384]{2,1,0:T(1,128)} %scale_ref.3) | copy-start | bytes 4612
  0.6 28.5 %copy-start.6 = (s32[1,1,384]{2,1,0:T(1,128)S(1)}, s32[1,1,384]{2,1,0:T(1,128)}, u32[]{:S(2)}) copy-start(s32[1,1,384]{2,1,0:T(1,128)} %cols_ref.3) | copy-start | bytes 4612
  0.7 28.5 %copy-start.5 = (s32[1,1,384]{2,1,0:T(1,128)S(1)}, s32[1,1,384]{2,1,0:T(1,128)}, u32[]{:S(2)}) copy-start(s32[1,1,384]{2,1,0:T(1,128)} %rows_ref.3) | copy-start | bytes 4612
  29.2 1.3 %copy-start = (bf16[8,4,160,128]{3,2,1,0:T(8,128)(2,1)S(1)}, bf16[8,4,160,128]{3,2,1,0:T(8,128)(2,1)}, u32[]{:S(2)}) copy-start(bf16[8,4,160,128]{3,2,1,0:T(8,128)(2,1)} %spread.1) | copy-start | bytes 3932164
  30.5 8.2 %copy-start.2 = (f32[4096]{0:T(1024)S(1)}, f32[4096]{0:T(1024)}, u32[]{:S(2)}) copy-start(f32[4096]{0:T(1024)} %param.16) | copy-start | bytes 49156
  51.1 7.1 %copy-start.3 = (s32[512]{0:T(512)S(1)}, s32[512]{0:T(512)}, u32[]{:S(2)}) copy-start(s32[512]{0:T(512)} %lat_ref.3) | copy-start | bytes 6148
  51.1 7.1 %copy-start.4 = (s32[512]{0:T(512)S(1)}, s32[512]{0:T(512)}, u32[]{:S(2)}) copy-start(s32[512]{0:T(512)} %lon_ref.3) | copy-start | bytes 6148
  58.2 41.1 %copy-start.1 = (f32[8,4,32,640]{3,2,1,0:T(8,128)S(1)}, f32[8,4,32,640]{3,2,1,0:T(8,128)}, u32[]{:S(2)}) copy-start(f32[8,4,32,640]{3,2,1,0:T(8,128)} %solution_ref.1) | copy-start | bytes 7864324
